TPU v7x, 512 devices: a whole 4x4x16 slice. The times are simulated.
512 devices in a mesh: nodes: 64 (over x, z), heads: 8 (over y, core).
Axes of the slice: x: 4, y: 4, z: 16, core: 2. Of those that a mesh axis runs over, the one named last changes fastest.
Arguments:
- hidden: bfloat16 [64, 7168], P('nodes'), may hold values from -6 to 6
- norm_gain: float32 [7168], replicated, may hold values from 0.1 to 1.9
- qkv_weight: bfloat16 [7168, 56, 384], P('nodes', 'heads'), may hold values from -0.0625 to 0.0625
- out_weight: bfloat16 [7168, 7168], P('heads', 'nodes'), may hold values from -0.0625 to 0.0625
- prefix_keys: bfloat16 [256, 128, 56, 128], P('nodes', None, 'heads'), may hold values from -1000 to 1000
- prefix_values: bfloat16 [256, 128, 56, 128], P('nodes', None, 'heads'), may hold values from -3 to 3
- leaf_keys: bfloat16 [64, 64, 56, 128], P('nodes', None, 'heads'), may hold values from -1000 to 1000
- leaf_values: bfloat16 [64, 64, 56, 128], P('nodes', None, 'heads'), may hold values from -3 to 3
- piece_node: int32 [256], replicated, may hold values from 0 to 35, as said below
- mid_parent: int32 [32], replicated, may hold values from 0 to 3
- leaf_parent: int32 [64], replicated, may hold values from 0 to 31
- leaf_len: int32 [64], replicated, may hold values from 1 to 64
- sink_len: int32 [64], replicated, may hold values from 0 to 4
- window_len: int32 [64], replicated, may hold values from 2048 to 4096
Outputs:
- layer_out: bfloat16 [64, 7168], P('heads', 'nodes')
Inputs may be any that keep to these rules, and one draw needn't show every extreme that they name: `piece_node`: every root owns some pieces; a middle node may own none.
All inputs are finite; a program needn't handle non-finite values.
Results may differ from a plain program's by a relative error of at most 0.007.
The roundings to bfloat16 on the way count: a program that leaves them out, or rounds other values in their place, can miss the bound.
Values may be sent and summed in bfloat16 or wider, within the bound.
A program may use at most 64 MiB of HBM per device.

v0:
```python
import math

import jax
import jax.numpy as jnp
from jax import lax
from jax.sharding import PartitionSpec as P

SEG = 128
ROOTS = 4
MIDS = 32


epsilon = 1e-05
negative_fill = -1e30


def joined(part, axis, combine):
    gathered = jax.tree.map(lambda a: lax.all_gather(a, axis), part)

    def take(source):
        return jax.tree.map(lambda a: lax.dynamic_index_in_dim(a, source, 0, False), gathered)

    return lax.fori_loop(
        1, lax.axis_size(axis), lambda source, state: combine(state, take(source)), take(0)
    )


def layer_norm(hidden, norm_gain):
    values = hidden.astype(jnp.float32)
    mean_value = jnp.mean(values, axis=1, keepdims=True)
    centered = values - mean_value
    variance = jnp.mean(centered * centered, axis=1, keepdims=True)
    return (centered * lax.rsqrt(variance + epsilon) * norm_gain[None, :]).astype(jnp.bfloat16)


def lookup(lookup_table, chosen):
    positions = jnp.arange(lookup_table.shape[0], dtype=jnp.int32)
    picked = jnp.where(chosen[:, None] == positions[None, :], lookup_table[None, :], 0)
    return jnp.sum(picked, axis=1)


def tree_rows(piece_node, mid_parent, leaf_parent, leaf_len):
    node_ids = jnp.arange(ROOTS + MIDS, dtype=jnp.int32)
    counts = jnp.sum((piece_node[:, None] == node_ids[None, :]).astype(jnp.int32), axis=0)
    root_node = lookup(mid_parent, leaf_parent)
    mid_node = leaf_parent + ROOTS
    root_len = SEG * lookup(counts, root_node)
    mid_len = SEG * lookup(counts, mid_node)
    finish = root_len + mid_len + leaf_len
    return (root_node, mid_node, root_len, finish)


def piece_rank(piece_node, chosen):
    all_pieces = jnp.arange(piece_node.shape[0], dtype=jnp.int32)
    nodes_here = lookup(piece_node, chosen)
    same = (piece_node[None, :] == nodes_here[:, None]) & (all_pieces[None, :] < chosen[:, None])
    return (nodes_here, jnp.sum(same.astype(jnp.int32), axis=1))


def prefix_allowed(
    node_block, rank_block, root_node, mid_node, root_len, finish, sink_len, window_len
):
    offsets = jnp.arange(SEG, dtype=jnp.int32)
    rel_pos = rank_block[:, None] * SEG + offsets[None, :]
    at_root = node_block[None, :] == root_node[:, None]
    at_mid = node_block[None, :] == mid_node[:, None]
    token_pos = rel_pos[None, :, :] + jnp.where(at_mid, root_len[:, None], 0)[:, :, None]
    inside = (token_pos < sink_len[:, None, None]) | (
        token_pos >= (finish - window_len)[:, None, None]
    )
    return ((at_root | at_mid)[:, :, None] & inside)[:, None, :, :]


def leaf_allowed(finish, leaf_len, sink_len, window_len, leaf_max):
    offsets = jnp.arange(leaf_max, dtype=jnp.int32)
    token_pos = (finish - leaf_len)[:, None] + offsets[None, :]
    inside = (token_pos < sink_len[:, None]) | (token_pos >= (finish - window_len)[:, None])
    return (inside & (offsets[None, :] < leaf_len[:, None]))[:, None, :]


def combine(first_part, second_part):
    highest = jnp.maximum(first_part[0], second_part[0])
    factor_one = jnp.exp(first_part[0] - highest)
    factor_two = jnp.exp(second_part[0] - highest)
    totals = first_part[1] * factor_one + second_part[1] * factor_two
    summed = first_part[2] * factor_one[..., None] + second_part[2] * factor_two[..., None]
    return (highest, totals, summed)


def weigh(scores, allowed, axes):
    masked = jnp.where(allowed, scores, negative_fill)
    maxima = jnp.max(masked, axis=axes)
    expanded = maxima
    for axis_pos in axes:
        expanded = jnp.expand_dims(expanded, axis_pos)
    weights = jnp.where(allowed, jnp.exp(masked - expanded), 0.0).astype(jnp.bfloat16)
    return (maxima, weights)


def on_device(
    hidden,
    norm_gain,
    qkv_weight,
    out_weight,
    prefix_keys,
    prefix_values,
    leaf_keys,
    leaf_values,
    piece_node,
    mid_parent,
    leaf_parent,
    leaf_len,
    sink_len,
    window_len,
):
    node_index = lax.axis_index("nodes")
    req_dev = hidden.shape[0]
    heads_dev = qkv_weight.shape[1]
    head_size = qkv_weight.shape[2] // 3
    seg_dev = prefix_keys.shape[0]
    first_row = node_index * req_dev
    score_scale = 1.0 / math.sqrt(head_size)
    normed = layer_norm(hidden, norm_gain)
    columns = lax.all_to_all(normed, "nodes", split_axis=1, concat_axis=0, tiled=True)
    width_here = columns.shape[1]
    flat_weight = qkv_weight.reshape(width_here, heads_dev * 3 * head_size)
    mixed_rows = lax.psum_scatter(
        jnp.dot(columns, flat_weight, preferred_element_type=jnp.float32),
        "nodes",
        scatter_dimension=0,
        tiled=True,
    )
    mixed_rows = mixed_rows.astype(jnp.bfloat16).reshape(req_dev, heads_dev, 3, head_size)
    query_here = mixed_rows[:, :, 0]
    key_new = mixed_rows[:, :, 1]
    value_new = mixed_rows[:, :, 2]
    query_all = lax.all_gather(query_here, "nodes", axis=0, tiled=True)
    root_node, mid_node, root_len, finish = tree_rows(piece_node, mid_parent, leaf_parent, leaf_len)
    chosen = node_index * seg_dev + jnp.arange(seg_dev, dtype=jnp.int32)
    node_block, rank_block = piece_rank(piece_node, chosen)
    scores = (
        jnp.einsum("rhd,pshd->rhps", query_all, prefix_keys, preferred_element_type=jnp.float32)
        * score_scale
    )
    allowed = prefix_allowed(
        node_block, rank_block, root_node, mid_node, root_len, finish, sink_len, window_len
    )
    maxima, weights = weigh(scores, allowed, (2, 3))
    totals = jnp.sum(weights.astype(jnp.float32), axis=(2, 3))
    summed = jnp.einsum(
        "rhps,pshd->rhd", weights, prefix_values, preferred_element_type=jnp.float32
    )
    merged = joined((maxima, totals, summed), "nodes", combine)
    merged = tuple((lax.dynamic_slice_in_dim(member, first_row, req_dev, 0) for member in merged))
    finish_here = lax.dynamic_slice_in_dim(finish, first_row, req_dev, 0)
    leaf_here = lax.dynamic_slice_in_dim(leaf_len, first_row, req_dev, 0)
    sink_here = lax.dynamic_slice_in_dim(sink_len, first_row, req_dev, 0)
    window_here = lax.dynamic_slice_in_dim(window_len, first_row, req_dev, 0)
    leaf_scores = (
        jnp.einsum("rhd,rjhd->rhj", query_here, leaf_keys, preferred_element_type=jnp.float32)
        * score_scale
    )
    leaf_mask = leaf_allowed(finish_here, leaf_here, sink_here, window_here, leaf_keys.shape[1])
    leaf_max, leaf_weights = weigh(leaf_scores, leaf_mask, (2,))
    leaf_part = (
        leaf_max,
        jnp.sum(leaf_weights.astype(jnp.float32), axis=2),
        jnp.einsum("rhj,rjhd->rhd", leaf_weights, leaf_values, preferred_element_type=jnp.float32),
    )
    own_score = (
        jnp.sum(query_here.astype(jnp.float32) * key_new.astype(jnp.float32), axis=2) * score_scale
    )
    own_part = (
        own_score,
        jnp.ones((req_dev, heads_dev), jnp.float32),
        value_new.astype(jnp.float32),
    )
    merged = combine(combine(merged, leaf_part), own_part)
    attended = (
        (merged[2] / merged[1][..., None])
        .astype(jnp.bfloat16)
        .reshape(req_dev, heads_dev * head_size)
    )
    out_rows = jnp.dot(
        lax.all_gather(attended, "nodes", axis=0, tiled=True),
        out_weight,
        preferred_element_type=jnp.float32,
    )
    return lax.psum_scatter(out_rows, "heads", scatter_dimension=0, tiled=True).astype(jnp.bfloat16)


def solution(mesh):
    return jax.shard_map(
        on_device,
        mesh=mesh,
        in_specs=(
            P("nodes", None),
            P(),
            P("nodes", "heads", None),
            P("heads", "nodes"),
            P("nodes", None, "heads", None),
            P("nodes", None, "heads", None),
            P("nodes", None, "heads", None),
            P("nodes", None, "heads", None),
            P(),
            P(),
            P(),
            P(),
            P(),
            P(),
        ),
        out_specs=P("heads", "nodes"),
        check_vma=False,
    )
```

profile of v0, /device:TPU:1, one launch (start us, length us, event | category | flops | bytes accessed | tf_op | source)
XLA Modules:
  0.0 809.0 jit_solution(8103925422148323476)
XLA Ops:
  6.5 1.5 convert_reduce_fusion.3
  8.7 1.4 multiply_reduce_fusion
  12.4 19.1 %all-to-all-start = ((bf16[1,64,112]{2,0,1:T(2,128)(2,1)}), bf16[1,64,112]{2,0,1:T(2,128)(2,1)S(1)}, u32[]{:S(2)}, u32[]{:S(2)}) async-start(bf16[1,64,112]{2,0,1:T(2,128)(2,1)} %all_to_all.15), calls=%async_computation | async-start | bytes 65536 | tf_op jit(solution)/shard_map/all_to_all | solution.py:124
  37.3 1.1 copy.86
  38.5 1.3 dynamic-slice
  39.7 5.1 all-to-all-done
  45.0 226.4 %all-reduce.3 = bf16[64,2688]{1,0:T(8,128)(2,1)S(1)} all-reduce(f32[64,2688]{1,0:T(8,128)S(1)} %fusion.19), channel_id=6, replica_groups=mesh['nodes'=64,'heads'=8] {'nodes'}, use_global_device_ids=true, to_apply=%region_8.9.clone | all-reduce | flops 172032 | bytes 1032192
  272.1 71.1 %all-gather = bf16[64,7,1,128]{3,1,2,0:T(8,128)(2,1)S(1)} all-gather(bf16[1,7,1,128]{3,1,2,0:T(8,128)(2,1)S(1)} %copy.68), channel_id=2, replica_groups=mesh['nodes'=64,'heads'=8] {'nodes'}, dimensions={0}, use_global_device_ids=true | all-gather | bytes 116480 | tf_op jit(solution)/shard_map/all_gather | solution.py:137
  343.7 2.2 convolution_bitcast_fusion
  346.0 1.2 dynamic_slice.68
  347.2 1.3 dynamic_slice.70
  348.5 1.3 dynamic_slice.69
  352.9 1.3 dynamic-slice.2
  354.9 1.3 compare_and_fusion
  356.2 64.2 %all-gather.4 = f32[64,64,7]{1,2,0:T(8,128)S(1)} all-gather(f32[1,64,7]{1,2,0:T(8,128)S(1)} %bitcast.134), channel_id=3, replica_groups=mesh['nodes'=64,'heads'=8] {'nodes'}, dimensions={0}, use_global_device_ids=true | all-gather | bytes 116480 | tf_op jit(solution)/shard_map/all_gather | solution.py:18
  420.7 64.7 %all-gather.5 = f32[64,64,7]{1,2,0:T(8,128)S(1)} all-gather(f32[1,64,7]{1,2,0:T(8,128)S(1)} %bitcast.136), channel_id=4, replica_groups=mesh['nodes'=64,'heads'=8] {'nodes'}, dimensions={0}, use_global_device_ids=true | all-gather | bytes 116480 | tf_op jit(solution)/shard_map/all_gather | solution.py:18
  485.4 1.1 fusion.16
  487.0 1.0 fusion.14
  488.0 114.8 %all-gather.9.cloned.1.call-done = f32[4096,7,128]{2,0,1:T(8,128)} async-done(((f32[64,7,128]{2,0,1:T(8,128)}), f32[4096,7,128]{2,0,1:T(8,128)}) %all-gather.9.cloned.1.call-update) | async-done | bytes 14680080 | tf_op jit(solution)/shard_map/all_gather | solution.py:18
  603.9 95.5 %while.19 = (s32[]{:T(128)}, f32[64,7]{0,1:T(8,128)S(1)}, f32[64,7]{0,1:T(8,128)S(1)}, f32[64,7,128]{2,1,0:T(8,128)S(1)}, f32[64,64,7]{1,2,0:T(8,128)S(1)}, /*in...) while((s32[]{:T(128)}, f32[64,7]{0,1:T(8,128)S(1)}, ...), condition=%wide.region_12.13_spmd, body=%wide.region_11.12_spmd.sunk | while | flops 174725 | bytes 1172119 | solution.py:23
  605.5 1.0 constant_dynamic-slice_fusion.4
  608.5 1.0 constant_dynamic-slice_fusion.4
  611.5 1.0 constant_dynamic-slice_fusion.4
  614.6 1.0 constant_dynamic-slice_fusion.4
  619.1 1.0 constant_dynamic-slice_fusion.4
  622.1 1.0 constant_dynamic-slice_fusion.4
  625.2 1.0 constant_dynamic-slice_fusion.4
  628.2 1.0 constant_dynamic-slice_fusion.4
  631.2 1.0 constant_dynamic-slice_fusion.4
  634.3 1.0 constant_dynamic-slice_fusion.4
  637.3 1.0 constant_dynamic-slice_fusion.4
  640.3 1.0 constant_dynamic-slice_fusion.4
  643.4 1.0 constant_dynamic-slice_fusion.4
  647.9 1.0 constant_dynamic-slice_fusion.4
  650.9 1.0 constant_dynamic-slice_fusion.4
  654.0 1.0 constant_dynamic-slice_fusion.4
  657.0 1.0 constant_dynamic-slice_fusion.4
  660.0 1.0 constant_dynamic-slice_fusion.4
  663.1 1.0 constant_dynamic-slice_fusion.4
  666.1 1.0 constant_dynamic-slice_fusion.4
  669.1 1.0 constant_dynamic-slice_fusion.4
  672.2 1.0 constant_dynamic-slice_fusion.4
  676.7 1.0 constant_dynamic-slice_fusion.4
  679.7 1.0 constant_dynamic-slice_fusion.4
  682.8 1.0 constant_dynamic-slice_fusion.4
  685.8 1.0 constant_dynamic-slice_fusion.4
  699.9 62.0 %all-gather.6 = bf16[64,1,896]{2,1,0:T(2,128)(2,1)S(1)} all-gather(bf16[1,1,896]{2,1,0:T(2,128)(2,1)S(1)} %convert_bitcast_fusion), channel_id=1, replica_groups=mesh['nodes'=64,'heads'=8] {'nodes'}, dimensions={0}, use_global_device_ids=true | all-gather | bytes 116480 | tf_op jit(solution)/shard_map/all_gather | solution.py:185
  762.1 39.5 %all-reduce.1 = bf16[64,112]{1,0:T(8,128)(2,1)S(1)} all-reduce(f32[64,112]{1,0:T(8,128)S(1)} %fusion.10), channel_id=7, replica_groups=mesh['nodes'=64,'heads'=8] {'heads'}, use_global_device_ids=true, to_apply=%region_16.17.clone | all-reduce | flops 7168 | bytes 43008
  (334 shorter events, 80.7 us)
Async XLA Ops:
  6.5 336.7 %copy-start = (bf16[4,128,7,128]{3,1,2,0:T(8,128)(2,1)S(1)}, bf16[4,128,7,128]{3,1,2,0:T(8,128)(2,1)}, u32[]{:S(2)}) copy-start(bf16[4,128,7,128]{3,1,2,0:T(8,128)(2,1)} %param.20) | copy-start | bytes 2752516
  6.5 755.3 %copy-start.1 = (bf16[896,112]{0,1:T(8,128)(2,1)S(1)}, bf16[896,112]{0,1:T(8,128)(2,1)}, u32[]{:S(2)}) copy-start(bf16[896,112]{0,1:T(8,128)(2,1)} %param.19) | copy-start | bytes 602116
  12.4 32.4 %all-to-all-start = ((bf16[1,64,112]{2,0,1:T(2,128)(2,1)}), bf16[1,64,112]{2,0,1:T(2,128)(2,1)S(1)}, u32[]{:S(2)}, u32[]{:S(2)}) async-start(bf16[1,64,112]{2,0,1:T(2,128)(2,1)} %all_to_all.15), calls=%async_computation | async-start | bytes 65536 | tf_op jit(solution)/shard_map/all_to_all | solution.py:124
  31.5 571.3 %all-gather.9.cloned.1.call-start = ((), (), s32[]{:S(2)}) async-start(), calls=%async_computation.1 | async-start | bytes 14909440 | tf_op jit(solution)/shard_map/all_gather | solution.py:18
Sparse Core Ops, SparseCore 0:
  346.1 256.6 all-gather.8
where the time goes:
time: 813 us; the launch traced here: 809 us
  blocking collectives  528 us (65%)
  waiting for transfers between devices  120 us (15%)
  local copies, waits for them, and re-layouts  84.4 us (10%)
  other arithmetic  32.2 us (4%)
  starting transfers between devices  19.2 us (2%)
  between operations  18 us (2%)
    unnamed x2, blocking collectives  266 us
    all_gather x2, blocking collectives, joined(): gathered = jax.tree.map(lambda a: lax.all_gather(a, axis), part)  129 us
    all_gather x1, waiting for transfers between devices, joined(): gathered = jax.tree.map(lambda a: lax.all_gather(a, axis), part)  115 us
    all_gather x1, blocking collectives, on_device(): query_all = lax.all_gather(query_here, 'nodes', axis=0, tiled=True)  71.1 us
    all_gather x1, blocking collectives, on_device(): lax.all_gather(attended, 'nodes', axis=0, tiled=True)  62 us
    dynamic_slice x66, local copies, waits for them, and re-layouts, take(): lax.dynamic_index_in_dim(a, source, 0, False)  61.8 us
    add x63, other arithmetic, combine(): first_part[2] * factor_one[..., None]  19.3 us
    all_to_all x1, starting transfers between devices, on_device(): lax.all_to_all(normed, 'nodes', split_axis=1, concat_axis=0, tiled=True)  19.1 us
  transfers between devices with their start and end apart: 2, of which 2 were waited for; matrix products, arithmetic and copies ran while one was open for 2% of the time, Pallas kernels for 0%

commit v1 on v0

v1 whole, which is shorter than its diff:
```python
import functools
import math

import jax
import jax.numpy as jnp
from jax import lax
from jax.experimental import pallas as pl
from jax.experimental.pallas import tpu as pltpu
from jax.sharding import PartitionSpec as P

MESH = pl.DeviceIdType.MESH
F32 = jnp.float32
BF16 = jnp.bfloat16
ROOTS = 4
EPSILON = 1e-05
NEGATIVE = -1e30
ZS = 16


def column(row):
    n = row.shape[1]
    here = lax.broadcasted_iota(jnp.int32, (n, n), 0) == lax.broadcasted_iota(jnp.int32, (n, n), 1)
    return jnp.sum(jnp.where(here, jnp.broadcast_to(row, (n, n)), 0.0), axis=1, keepdims=True)


def dot_t(a, b):
    return lax.dot_general(a, b, (((1,), (1,)), ((), ())), preferred_element_type=F32)


def dot(a, b):
    return jnp.dot(a, b, preferred_element_type=F32)


def kernel(dims, names, *refs):
    nodes, heads_n, heads, head_size, width, seg_dev, seg, leaf_max, out_width = dims
    r = dict(zip(names, refs, strict=True))
    xs = nodes // ZS
    me = lax.axis_index("nodes")
    hd = lax.axis_index("heads")
    x, z = me // ZS, lax.rem(me, ZS)
    scale = 1.0 / math.sqrt(head_size)

    def at_x(dx):
        return {"nodes": lax.rem(x + dx, xs) * ZS + z, "heads": hd}

    def far(j):
        half = (j + 1) // 2
        return lax.rem(z + ZS // 2 + half * (1 - 2 * lax.rem(j, 2)), ZS)

    def at_z(tz):
        return {"nodes": x * ZS + tz, "heads": hd}

    def at_h(dh):
        return {"nodes": me, "heads": lax.rem(hd + dh, heads_n)}

    def remote(src, dst, sem, target):
        return pltpu.make_async_remote_copy(
            src_ref=src,
            dst_ref=dst,
            send_sem=r["send"].at[sem],
            recv_sem=r["recv"].at[sem],
            device_id=target,
            device_id_type=MESH,
        )

    barrier = pltpu.get_barrier_semaphore()

    def tell(target):
        pl.semaphore_signal(barrier, inc=1, device_id=target, device_id_type=MESH)

    @pl.loop(0, ZS - 1)
    def _(j):
        tell(at_z(far(j)))

    for dx in range(1, xs):
        tell(at_x(dx))
    for dh in range(1, heads_n):
        tell(at_h(dh))

    loads = [
        pltpu.make_async_copy(r[n + "_hbm"], r[n], r["load"].at[i])
        for i, n in enumerate(("w", "k", "v", "lk", "lv", "wo"))
    ]
    for load in loads:
        load.start()

    values = r["hidden"][...].astype(F32)
    features = values.shape[1]
    mean = jnp.sum(values, axis=1, keepdims=True) * (1.0 / features)
    centered = values - mean
    variance = jnp.sum(centered * centered, axis=1, keepdims=True) * (1.0 / features)
    normed = centered * lax.rsqrt(variance + EPSILON) * r["gain"][...]
    normed = normed.astype(BF16).astype(F32)
    for n in range(nodes):
        r["rows"][n // ZS, n % ZS, :, pl.ds(0, width)] = normed[:, n * width : (n + 1) * width]

    pl.semaphore_wait(barrier, ZS - 1 + xs - 1 + heads_n - 1)

    rows, xrows, cols = r["rows"], r["xrows"], r["cols"]
    for dx in range(1, xs):
        tx = lax.rem(x + dx, xs)
        remote(rows.at[tx], xrows.at[x], 0, at_x(dx)).start()
    xrows[x] = rows[x]

    pn = r["pn"][...].astype(F32)
    pieces = pn.shape[1]
    mids = r["mp"].shape[1]
    parent = column(r["lp"][...].astype(F32))
    leaf_len = column(r["ll"][...].astype(F32))
    sink = column(r["sl"][...].astype(F32))
    window = column(r["wl"][...].astype(F32))
    mid_ids = lax.broadcasted_iota(jnp.int32, (nodes, mids), 1).astype(F32)
    mp = jnp.broadcast_to(r["mp"][...].astype(F32), (nodes, mids))
    root_node = jnp.sum(jnp.where(mid_ids == parent, mp, 0.0), axis=1, keepdims=True)
    mid_node = parent + float(ROOTS)
    pn_all = jnp.broadcast_to(pn, (nodes, pieces))
    root_len = float(seg) * jnp.sum(jnp.where(pn_all == root_node, 1.0, 0.0), axis=1, keepdims=True)
    mid_len = float(seg) * jnp.sum(jnp.where(pn_all == mid_node, 1.0, 0.0), axis=1, keepdims=True)
    finish = root_len + mid_len + leaf_len
    low = finish - window
    piece_ids = lax.broadcasted_iota(jnp.int32, (1, pieces), 1)
    offsets = lax.broadcasted_iota(jnp.int32, (nodes, seg), 1).astype(F32)
    for p in range(seg_dev):
        mine = me * seg_dev + p
        node = jnp.sum(jnp.where(piece_ids == mine, pn, 0.0), axis=1, keepdims=True)
        same = (pn == node) & (piece_ids < mine)
        rank = jnp.sum(jnp.where(same, 1.0, 0.0), axis=1, keepdims=True)
        at_mid = mid_node == node
        start = jnp.where(at_mid, root_len, 0.0) + rank * float(seg)
        position = offsets + start
        visible = ((position < sink) | (position >= low)) & (at_mid | (root_node == node))
        r["mask"][:, p * seg : (p + 1) * seg] = jnp.where(visible, 1.0, 0.0)
    my_row = lax.broadcasted_iota(jnp.int32, (nodes, 1), 0) == me

    def mine_of(values):
        return jnp.sum(jnp.where(my_row, values, 0.0), axis=0, keepdims=True)

    my_finish, my_leaf, my_sink = mine_of(finish), mine_of(leaf_len), mine_of(sink)
    my_low = mine_of(low)
    leaf_offsets = lax.broadcasted_iota(jnp.int32, (8, leaf_max), 1).astype(F32)
    leaf_position = leaf_offsets + (my_finish - my_leaf)
    leaf_visible = ((leaf_position < my_sink) | (leaf_position >= my_low)) & (leaf_offsets < my_leaf)
    r["leaf_mask"][...] = jnp.where(leaf_visible, 1.0, 0.0)

    remote(xrows.at[pl.ds(0, xs - 1)], xrows.at[pl.ds(0, xs - 1)], 0, at_x(1)).wait_recv()

    @pl.loop(0, ZS - 1)
    def _(j):
        tz = far(j)
        remote(xrows.at[:, tz], cols.at[:, z], 1, at_z(tz)).start()

    cols[:, z] = xrows[:, z]
    pq, pkv = r["pq"], r["pkv"]
    pq[:, heads, :] = jnp.zeros((nodes, head_size), F32)
    pkv[:, heads, :] = jnp.zeros((nodes, 2 * head_size), F32)
    loads[0].wait()
    some = pl.ds(0, ZS - 1)
    remote(cols.at[:, some], cols.at[:, some], 1, at_x(1)).wait_recv()

    lhs = jnp.concatenate([cols[i, :, 0, :] for i in range(xs)], axis=0)[:, :width].astype(BF16)
    for h in range(heads):
        pq[:, h, :] = dot(lhs, r["w"][h, :, pl.ds(0, head_size)])
    xq, sq, zq = r["xq"], r["sq"], r["zq"]
    for dx in range(1, xs):
        tx = lax.rem(x + dx, xs)
        remote(pq.at[pl.ds(tx * ZS, ZS)], xq.at[dx - 1], 2, at_x(dx)).start()
    for h in range(heads):
        pkv[:, h, :] = dot(lhs, r["w"][h, :, pl.ds(head_size, 2 * head_size)])
    remote(xq, xq, 2, at_x(1)).wait_recv()
    sq[...] = pq[pl.ds(x * ZS, ZS)] + xq[0] + xq[1] + xq[2]

    @pl.loop(0, ZS - 1)
    def _(j):
        tz = far(j)
        remote(sq.at[tz], zq.at[z], 3, at_z(tz)).start()

    xkv, skv, zkv = r["xkv"], r["skv"], r["zkv"]
    for dx in range(1, xs):
        tx = lax.rem(x + dx, xs)
        remote(pkv.at[pl.ds(tx * ZS, ZS)], xkv.at[dx - 1], 4, at_x(dx)).start()
    zq[z] = sq[z]
    remote(zq.at[some], zq.at[some], 3, at_x(1)).wait_recv()
    query = jnp.sum(zq[...], axis=0).astype(BF16)

    qa = r["qa"]
    qa[x, z] = query

    @pl.loop(0, ZS - 1)
    def _(j):
        remote(qa.at[x, z], qa.at[x, z], 5, at_z(far(j))).start()

    remote(xkv, xkv, 4, at_x(1)).wait_recv()
    skv[...] = pkv[pl.ds(x * ZS, ZS)] + xkv[0] + xkv[1] + xkv[2]
    remote(qa.at[0, some], qa.at[0, some], 5, at_x(1)).wait_recv()
    for dx in range(1, xs):
        remote(qa.at[x], qa.at[x], 6, at_x(dx)).start()

    @pl.loop(0, ZS - 1)
    def _(j):
        tz = far(j)
        remote(skv.at[tz], zkv.at[z], 7, at_z(tz)).start()

    zkv[z] = skv[z]

    row_ids = lax.broadcasted_iota(jnp.int32, (8, 1), 0)
    loads[3].wait()
    loads[4].wait()
    leaf_scores = jnp.zeros((8, leaf_max), F32)
    for h in range(heads):
        leaf_scores = jnp.where(row_ids == h, dot_t(query, r["lk"][h]), leaf_scores)
    leaf_on = r["leaf_mask"][...] > 0.0
    leaf_scores = jnp.where(leaf_on, leaf_scores * scale, NEGATIVE)
    leaf_m = jnp.max(leaf_scores, axis=1, keepdims=True)
    leaf_w = jnp.where(leaf_on, jnp.exp(leaf_scores - leaf_m), 0.0).astype(BF16)
    leaf_l = jnp.sum(leaf_w.astype(F32), axis=1, keepdims=True)
    leaf_n = jnp.zeros((8, head_size), F32)
    for h in range(heads):
        leaf_n = jnp.where(row_ids == h, dot(leaf_w, r["lv"][h]), leaf_n)

    loads[1].wait()
    loads[2].wait()
    three = pl.ds(0, xs - 1)
    remote(qa.at[three], qa.at[three], 6, at_x(1)).wait_recv()

    qf = r["qf"]
    qf[...] = qa[...].astype(F32).reshape(nodes, 8, head_size)
    lanes = lax.broadcasted_iota(jnp.int32, (nodes, 128), 1)
    stat_m = jnp.full((nodes, 128), NEGATIVE, F32)
    stat_l = jnp.zeros((nodes, 128), F32)
    nb, st = r["nb"], r["st"]
    for h in range(heads):
        qh = qf[:, h, :].astype(BF16)
        on = r["mask"][...] > 0.0
        scores = jnp.concatenate([dot_t(qh, r["k"][p, h]) for p in range(seg_dev)], axis=1)
        scores = jnp.where(on, scores * scale, NEGATIVE)
        top = jnp.max(scores, axis=1, keepdims=True)
        weights = jnp.where(on, jnp.exp(scores - top), 0.0).astype(BF16)
        total = jnp.sum(weights.astype(F32), axis=1, keepdims=True)
        summed = dot(weights[:, :seg], r["v"][0, h])
        for p in range(1, seg_dev):
            summed = summed + dot(weights[:, p * seg : (p + 1) * seg], r["v"][p, h])
        nb[:, h] = summed.astype(BF16).reshape(xs, ZS, head_size)
        stat_m = jnp.where(lanes == h, top, stat_m)
        stat_l = jnp.where(lanes == h, total, stat_l)
    st[:, 0] = stat_m.reshape(xs, ZS, 128)
    st[:, 1] = stat_l.reshape(xs, ZS, 128)

    xn, xst = r["xn"], r["xst"]
    for dx in range(1, xs):
        tx = lax.rem(x + dx, xs)
        remote(nb.at[tx], xn.at[dx - 1], 8, at_x(dx)).start()
        remote(st.at[tx], xst.at[dx - 1], 9, at_x(dx)).start()
    remote(xn, xn, 8, at_x(1)).wait_recv()
    remote(xst, xst, 9, at_x(1)).wait_recv()
    ms = [st[x, 0]] + [xst[i, 0] for i in range(xs - 1)]
    ls = [st[x, 1]] + [xst[i, 1] for i in range(xs - 1)]
    top = functools.reduce(jnp.maximum, ms)
    factors = [jnp.exp(m - top) for m in ms]
    total = functools.reduce(jnp.add, [f * t for f, t in zip(factors, ls, strict=True)])
    zs, zn, zn32, tn, ts = r["zs"], r["zn"], r["zn32"], r["tn"], r["ts"]
    zs[:, 0, :] = top
    zs[:, 1, :] = total
    for h in range(heads):
        parts = [nb[x, h]] + [xn[i, h] for i in range(xs - 1)]
        terms = [f[:, h : h + 1] * p.astype(F32) for f, p in zip(factors, parts, strict=True)]
        zn32[:, h, :] = functools.reduce(jnp.add, terms)
    zn32[:, heads, :] = jnp.zeros((ZS, head_size), F32)
    zn[...] = zn32[...].astype(BF16)

    @pl.loop(0, ZS - 1)
    def _(j):
        tz = far(j)
        remote(zn.at[tz], tn.at[z], 10, at_z(tz)).start()
        remote(zs.at[tz], ts.at[z], 11, at_z(tz)).start()

    tn[z] = zn[z]
    ts[z] = zs[z]

    remote(zkv.at[some], zkv.at[some], 7, at_x(1)).wait_recv()
    new = jnp.sum(zkv[...], axis=0).astype(BF16).astype(F32)
    own_m = jnp.sum(query.astype(F32) * new[:, :head_size], axis=1, keepdims=True) * scale
    own_n = new[:, head_size:]

    remote(tn.at[some], tn.at[some], 10, at_x(1)).wait_recv()
    remote(ts.at[some], ts.at[some], 11, at_x(1)).wait_recv()
    diagonal = lax.broadcasted_iota(jnp.int32, (8, 128), 0) == lax.broadcasted_iota(
        jnp.int32, (8, 128), 1
    )

    def stat(i, which):
        row = jnp.broadcast_to(ts[i, which : which + 1, :], (8, 128))
        return jnp.sum(jnp.where(diagonal, row, 0.0), axis=1, keepdims=True)

    ms = [stat(i, 0) for i in range(ZS)]
    top = functools.reduce(jnp.maximum, ms + [leaf_m, own_m])
    own_f = jnp.exp(own_m - top)
    leaf_f = jnp.exp(leaf_m - top)
    total = own_f + leaf_f * leaf_l
    summed = own_f * own_n + leaf_f * leaf_n
    for i in range(ZS):
        f = jnp.exp(ms[i] - top)
        total = total + f * stat(i, 1)
        summed = summed + f * tn[i].astype(F32)
    attended = (summed / total).astype(BF16)

    aa = r["aa"]
    aa[x, z] = attended

    @pl.loop(0, ZS - 1)
    def _(j):
        remote(aa.at[x, z], aa.at[x, z], 12, at_z(far(j))).start()

    loads[5].wait()
    remote(aa.at[0, some], aa.at[0, some], 12, at_x(1)).wait_recv()
    for dx in range(1, xs):
        remote(aa.at[x], aa.at[x], 13, at_x(dx)).start()
    remote(aa.at[three], aa.at[three], 13, at_x(1)).wait_recv()

    qf[...] = aa[...].astype(F32).reshape(nodes, 8, head_size)
    acc = jnp.zeros((nodes, out_width), F32)
    for h in range(heads):
        acc = acc + dot_t(qf[:, h, :].astype(BF16), r["wo"][:, h * head_size : (h + 1) * head_size])
    rows_out = nodes // heads_n
    os, orr = r["os"], r["orr"]
    os[:, :, pl.ds(0, out_width)] = acc.reshape(heads_n, rows_out, out_width)
    for dh in range(1, heads_n):
        remote(os.at[lax.rem(hd + dh, heads_n)], orr.at[dh - 1], 14, at_h(dh)).start()
    remote(orr, orr, 14, at_x(1)).wait_recv()
    result = os[hd] + jnp.sum(orr[...], axis=0)
    r["out"][...] = result[:, :out_width].astype(BF16)

    for sem, ref in (
        (0, xrows.at[three]),
        (1, cols.at[:, some]),
        (2, xq),
        (3, zq.at[some]),
        (4, xkv),
        (5, qa.at[0, some]),
        (6, qa.at[three]),
        (7, zkv.at[some]),
        (8, xn),
        (9, xst),
        (10, tn.at[some]),
        (11, ts.at[some]),
        (12, aa.at[0, some]),
        (13, aa.at[three]),
        (14, orr),
    ):
        remote(ref, ref, sem, at_x(1)).wait_send()


def on_device(
    hidden,
    norm_gain,
    qkv_weight,
    out_weight,
    prefix_keys,
    prefix_values,
    leaf_keys,
    leaf_values,
    piece_node,
    mid_parent,
    leaf_parent,
    leaf_len,
    sink_len,
    window_len,
):
    nodes = lax.axis_size("nodes")
    heads_n = lax.axis_size("heads")
    xs = nodes // ZS
    width, heads, triple = qkv_weight.shape
    head_size = triple // 3
    seg_dev, seg = prefix_keys.shape[:2]
    leaf_max = leaf_keys.shape[1]
    out_width = out_weight.shape[1]
    rows_out = nodes // heads_n
    dims = (nodes, heads_n, heads, head_size, width, seg_dev, seg, leaf_max, out_width)
    small = {
        "hidden": hidden,
        "gain": norm_gain[None, :],
        "pn": piece_node[None, :],
        "mp": mid_parent[None, :],
        "lp": leaf_parent[None, :],
        "ll": leaf_len[None, :],
        "sl": sink_len[None, :],
        "wl": window_len[None, :],
    }
    large = {
        "w_hbm": qkv_weight.transpose(1, 0, 2),
        "wo_hbm": out_weight.T,
        "k_hbm": prefix_keys.transpose(0, 2, 1, 3),
        "v_hbm": prefix_values.transpose(0, 2, 1, 3),
        "lk_hbm": leaf_keys[0].transpose(1, 0, 2),
        "lv_hbm": leaf_values[0].transpose(1, 0, 2),
    }
    vmem = pltpu.VMEM
    scratch = {n[:-4]: vmem(a.shape, a.dtype) for n, a in large.items()}
    scratch |= {
        "rows": vmem((xs, ZS, 1, 128), F32),
        "xrows": vmem((xs, ZS, 1, 128), F32),
        "cols": vmem((xs, ZS, 1, 128), F32),
        "mask": vmem((nodes, seg_dev * seg), F32),
        "leaf_mask": vmem((8, leaf_max), F32),
        "pq": vmem((nodes, 8, head_size), F32),
        "xq": vmem((xs - 1, ZS, 8, head_size), F32),
        "sq": vmem((ZS, 8, head_size), F32),
        "zq": vmem((ZS, 8, head_size), F32),
        "pkv": vmem((nodes, 8, 2 * head_size), F32),
        "xkv": vmem((xs - 1, ZS, 8, 2 * head_size), F32),
        "skv": vmem((ZS, 8, 2 * head_size), F32),
        "zkv": vmem((ZS, 8, 2 * head_size), F32),
        "qa": vmem((xs, ZS, 8, head_size), BF16),
        "aa": vmem((xs, ZS, 8, head_size), BF16),
        "qf": vmem((nodes, 8, head_size), F32),
        "nb": vmem((xs, heads, ZS, head_size), BF16),
        "xn": vmem((xs - 1, heads, ZS, head_size), BF16),
        "st": vmem((xs, 2, ZS, 128), F32),
        "xst": vmem((xs - 1, 2, ZS, 128), F32),
        "zn32": vmem((ZS, 8, head_size), F32),
        "zn": vmem((ZS, 8, head_size), BF16),
        "tn": vmem((ZS, 8, head_size), BF16),
        "zs": vmem((ZS, 2, 128), F32),
        "ts": vmem((ZS, 2, 128), F32),
        "os": vmem((heads_n, rows_out, 128), F32),
        "orr": vmem((heads_n - 1, rows_out, 128), F32),
        "load": pltpu.SemaphoreType.DMA((6,)),
        "send": pltpu.SemaphoreType.DMA((15,)),
        "recv": pltpu.SemaphoreType.DMA((15,)),
    }
    names = list(small) + list(large) + ["out"] + list(scratch)
    return pl.pallas_call(
        functools.partial(kernel, dims, names),
        out_shape=jax.ShapeDtypeStruct((rows_out, out_width), BF16),
        in_specs=[pl.BlockSpec(memory_space=pltpu.VMEM)] * len(small)
        + [pl.BlockSpec(memory_space=pl.ANY)] * len(large),
        out_specs=pl.BlockSpec(memory_space=pltpu.VMEM),
        scratch_shapes=list(scratch.values()),
        compiler_params=pltpu.CompilerParams(
            collective_id=0, has_side_effects=True, vmem_limit_bytes=60 * 2**20
        ),
    )(*small.values(), *large.values())


def solution(mesh):
    return jax.shard_map(
        on_device,
        mesh=mesh,
        in_specs=(
            P("nodes", None),
            P(),
            P("nodes", "heads", None),
            P("heads", "nodes"),
            P("nodes", None, "heads", None),
            P("nodes", None, "heads", None),
            P("nodes", None, "heads", None),
            P("nodes", None, "heads", None),
            P(),
            P(),
            P(),
            P(),
            P(),
            P(),
        ),
        out_specs=P("heads", "nodes"),
        check_vma=False,
    )
```

time: 813 us -> 83.6 us (0.10)
  blocking collectives: 528 us -> 0 us
  waiting for transfers between devices: 120 us -> 0 us
  local copies, waits for them, and re-layouts: 84.4 us -> 1.26 us
  Pallas kernels: 0 us -> 82.1 us
  other arithmetic: 32.2 us -> 0 us
  starting transfers between devices: 19.2 us -> 0 us
  between operations: 18 us -> 0.01 us
    unnamed x2 -> x0, blocking collectives: 266 us -> none
    all_gather x4 -> x0, blocking collectives: 262 us -> none  [the longest x2 129 us: joined(): gathered = jax.tree.map(lambda a: lax.all_gather(a, axis), part)]
    all_gather x1 -> x0, waiting for transfers between devices: 115 us -> none  [joined(): gathered = jax.tree.map(lambda a: lax.all_gather(a, axis), part)]
    pallas_call x0 -> x1, Pallas kernels: none -> 82.1 us  [on_device(): pl.pallas_call(functools.partial(kernel, dims, names), out_shape=jax.Shap...]
    dynamic_slice x70 -> x0, local copies, waits for them, and re-layouts: 66.3 us -> none  [the longest x66 61.8 us: take(): lax.dynamic_index_in_dim(a, source, 0, False)]
    add x129 -> x0, other arithmetic: 21.1 us -> none  [the longest x63 19.3 us: combine(): first_part[2] * factor_one[..., None]]
    all_to_all x1 -> x0, starting transfers between devices: 19.1 us -> none  [on_device(): lax.all_to_all(normed, 'nodes', split_axis=1, concat_axis=0, tiled=True)]
    exp x126 -> x0, local copies, waits for them, and re-layouts: 12.1 us -> none  [the longest x63 6.07 us: combine(): factor_two = jnp.exp(second_part[0] - highest)]
  transfers between devices with their start and end apart: 2 -> 0, of which waited for: 2 -> 0; matrix products, arithmetic and copies ran while one was open for 2% -> 0% of each run, Pallas kernels for 0% -> 0%
where the time goes in v1:
time: 83.6 us; the launch traced here: 83.4 us
  Pallas kernels  82.1 us (98%)
  local copies, waits for them, and re-layouts  1.26 us (2%)
    pallas_call x1, Pallas kernels, on_device(): pl.pallas_call(functools.partial(kernel, dims, names), out_shape=jax.Shap...  82.1 us

profile of v1, /device:TPU:1, one launch (start us, length us, event | category | flops | bytes accessed | tf_op | source)
XLA Modules:
  0.0 83.4 jit_solution(3284052501785534609)
XLA Ops:
  0.0 82.1 %shard_map.136 = bf16[8,112]{1,0:T(8,128)(2,1)} custom-call(bf16[1,7168]{1,0:T(2,128)(2,1)} %refs_0_.1, f32[1,7168]{1,0:T(1,128)} %bitcast.23, s32[1,256]{1,0:T(1,128)} %bitcast.24, s32[1,32]{1,0:T(1,128)} %bitcast.25, s32[1,64]{1,0:T(1,128)} %bitcast.26, s32[1,64]{1,0:T(1,128)} %bitcast.27, s32[1,64]{1,0:T(1,128)} %bitcast.28, s32[1,64]{1,0:T(1,128)} %bitcast.29, ...), custom_call_target="tpu_custom_call" | custom-call | tf_op jit(solution)/shard_map/pallas_call | solution.py:431
  82.1 1.3 %copy.16 = bf16[8,112]{1,0:T(8,128)(2,1)} copy(bf16[8,112]{1,0:T(8,128)(2,1)} %shard_map.136) | data formatting | bytes 3584

commit v2 on v1

v2 whole, which is shorter than its diff:
```python
import functools
import math

import jax
import jax.numpy as jnp
from jax import lax
from jax.experimental import pallas as pl
from jax.experimental.pallas import tpu as pltpu
from jax.sharding import PartitionSpec as P

MESH = pl.DeviceIdType.MESH
F32 = jnp.float32
BF16 = jnp.bfloat16
ROOTS = 4
EPSILON = 1e-05
NEGATIVE = -1e30
LOADED = ("hidden", "gain", "pn", "mp", "lp", "ll", "sl", "wl", "w", "k", "v", "lk", "lv", "wo")
ZS = 16


def rho(n):
    z = lax.rem(n, ZS) if not isinstance(n, int) else n % ZS
    return n - z + (z % 4) * 4 + z // 4


def column(row):
    n = row.shape[1]
    i = lax.broadcasted_iota(jnp.int32, (n, n), 0)
    here = (i // ZS) * ZS + (i % 4) * 4 + (i % ZS) // 4 == lax.broadcasted_iota(jnp.int32, (n, n), 1)
    return jnp.sum(jnp.where(here, jnp.broadcast_to(row, (n, n)), 0.0), axis=1, keepdims=True)


def dot_t(a, b):
    return lax.dot_general(a, b, (((1,), (1,)), ((), ())), preferred_element_type=F32)


def dot(a, b):
    return jnp.dot(a, b, preferred_element_type=F32)


def kernel(dims, names, *refs):
    nodes, heads_n, heads, head_size, width, seg_dev, seg, leaf_max, out_width = dims
    r = dict(zip(names, refs, strict=True))
    xs = nodes // ZS
    me = lax.axis_index("nodes")
    hd = lax.axis_index("heads")
    x, z = me // ZS, lax.rem(me, ZS)
    mine, block, turn = rho(me), x * 4 + lax.rem(z, 4), z // 4
    scale = 1.0 / math.sqrt(head_size)
    near = xs * 4 - 1
    owned = pl.ds(block * 4, 4)

    def at(tx, tz):
        return {"nodes": tx * ZS + tz, "heads": hd}

    def far(j):
        half = (j + 1) // 2
        return lax.rem(z + ZS // 2 + half * (1 - 2 * lax.rem(j, 2)), ZS)

    def across(j):
        return lax.rem(x + j, xs)

    def neighbour(j):
        i, k = lax.rem(j, 4), j // 4
        dx = 2 + ((i + 1) // 2) * (1 - 2 * lax.rem(i, 2))
        dz = 2 - k - k // 2 + 2 * (k // 3)
        return lax.rem(x + dx, xs), lax.rem(z + dz + ZS, ZS)

    def remote(src, dst, sem, target):
        return pltpu.make_async_remote_copy(
            src_ref=src,
            dst_ref=dst,
            send_sem=r["send"].at[sem],
            recv_sem=r["recv"].at[sem],
            device_id=target,
            device_id_type=MESH,
        )

    other = at(across(1), z)
    sent = []

    def arrive(sem, ref):
        remote(ref, ref, sem, other).wait_recv()
        sent.append((sem, ref))

    loads = {
        n: pltpu.make_async_copy(r[n + "_hbm"], r[n], r["load"].at[i])
        for i, n in enumerate(LOADED)
    }
    loads["hidden"].start()
    loads["gain"].start()
    barrier = pltpu.get_barrier_semaphore()

    def tell(target):
        pl.semaphore_signal(barrier, inc=1, device_id=target, device_id_type=MESH)

    @pl.loop(0, ZS - 1)
    def _(j):
        for dx in (2, 1, 3, 0):
            tell(at(across(dx), far(j)))

    for dx in range(1, xs):
        tell(at(across(dx), z))
    for dh in range(1, heads_n):
        tell({"nodes": me, "heads": lax.rem(hd + dh, heads_n)})

    for n in LOADED[2:]:
        loads[n].start()

    loads["hidden"].wait()
    loads["gain"].wait()
    values = r["hidden"][...].astype(F32)
    features = values.shape[1]
    mean = jnp.sum(values, axis=1, keepdims=True) * (1.0 / features)
    centered = values - mean
    variance = jnp.sum(centered * centered, axis=1, keepdims=True) * (1.0 / features)
    normed = centered * lax.rsqrt(variance + EPSILON) * r["gain"][...]
    normed = normed.astype(BF16).astype(F32)
    rows, cols = r["rows"], r["cols"]
    for n in range(nodes):
        rows[n, :, pl.ds(0, width)] = normed[:, n * width : (n + 1) * width]

    pl.semaphore_wait(barrier, nodes - 1 + heads_n - 1)

    @pl.loop(0, ZS - 1)
    def _(j):
        tz = far(j)
        for dx in (2, 1, 3, 0):
            tx = across(dx)
            remote(rows.at[tx * ZS + tz], cols.at[mine], 0, at(tx, tz)).start()

    for dx in range(1, xs):
        tx = across(dx)
        remote(rows.at[tx * ZS + z], cols.at[mine], 0, at(tx, z)).start()
    cols[mine] = rows[me]

    for n in ("pn", "mp", "lp", "ll", "sl", "wl"):
        loads[n].wait()
    pn = r["pn"][...].astype(F32)
    pieces = pn.shape[1]
    mids = r["mp"].shape[1]
    parent = column(r["lp"][...].astype(F32))
    leaf_len = column(r["ll"][...].astype(F32))
    sink = column(r["sl"][...].astype(F32))
    window = column(r["wl"][...].astype(F32))
    mid_ids = lax.broadcasted_iota(jnp.int32, (nodes, mids), 1).astype(F32)
    mp = jnp.broadcast_to(r["mp"][...].astype(F32), (nodes, mids))
    root_node = jnp.sum(jnp.where(mid_ids == parent, mp, 0.0), axis=1, keepdims=True)
    mid_node = parent + float(ROOTS)
    pn_all = jnp.broadcast_to(pn, (nodes, pieces))
    root_len = float(seg) * jnp.sum(jnp.where(pn_all == root_node, 1.0, 0.0), axis=1, keepdims=True)
    mid_len = float(seg) * jnp.sum(jnp.where(pn_all == mid_node, 1.0, 0.0), axis=1, keepdims=True)
    finish = root_len + mid_len + leaf_len
    low = finish - window
    piece_ids = lax.broadcasted_iota(jnp.int32, (1, pieces), 1)
    offsets = lax.broadcasted_iota(jnp.int32, (nodes, seg), 1).astype(F32)
    for p in range(seg_dev):
        here = me * seg_dev + p
        node = jnp.sum(jnp.where(piece_ids == here, pn, 0.0), axis=1, keepdims=True)
        same = (pn == node) & (piece_ids < here)
        rank = jnp.sum(jnp.where(same, 1.0, 0.0), axis=1, keepdims=True)
        at_mid = mid_node == node
        start = jnp.where(at_mid, root_len, 0.0) + rank * float(seg)
        position = offsets + start
        visible = ((position < sink) | (position >= low)) & (at_mid | (root_node == node))
        r["mask"][:, p * seg : (p + 1) * seg] = jnp.where(visible, 1.0, 0.0)
    my_row = lax.broadcasted_iota(jnp.int32, (nodes, 1), 0) == mine

    def mine_of(values):
        return jnp.sum(jnp.where(my_row, values, 0.0), axis=0, keepdims=True)

    my_finish, my_leaf, my_sink = mine_of(finish), mine_of(leaf_len), mine_of(sink)
    my_low = mine_of(low)
    leaf_offsets = lax.broadcasted_iota(jnp.int32, (8, leaf_max), 1).astype(F32)
    leaf_position = leaf_offsets + (my_finish - my_leaf)
    leaf_visible = ((leaf_position < my_sink) | (leaf_position >= my_low)) & (leaf_offsets < my_leaf)
    r["leaf_mask"][...] = jnp.where(leaf_visible, 1.0, 0.0)

    pq, pkv = r["pq"], r["pkv"]
    pq[:, heads, :] = jnp.zeros((nodes, head_size), F32)
    pkv[:, heads, :] = jnp.zeros((nodes, 2 * head_size), F32)
    loads["w"].wait()
    arrive(0, cols.at[pl.ds(0, nodes - 1)])

    lhs = cols[:, 0, :][:, :width].astype(BF16)
    for h in range(heads):
        pq[:, h, :] = dot(lhs, r["w"][h, :, pl.ds(0, head_size)])
    nq, fq = r["nq"], r["fq"]

    @pl.loop(0, near)
    def _(j):
        tx, tz = neighbour(j)
        src = pq.at[pl.ds((tx * 4 + lax.rem(tz, 4)) * 4, 4)]
        remote(src, nq.at[j], 1, at(tx, tz)).start()

    for h in range(heads):
        pkv[:, h, :] = dot(lhs, r["w"][h, :, pl.ds(head_size, 2 * head_size)])
    arrive(1, nq)
    fq[turn] = pq[owned] + jnp.sum(nq[...], axis=0)
    distant = [lax.rem(z + 4 * d, ZS) for d in (2, 1, 3)]
    for tz in distant:
        remote(fq.at[turn], fq.at[turn], 2, at(x, tz)).start()

    xkv, skv, nkv, tkv, fkv = r["xkv"], r["skv"], r["nkv"], r["tkv"], r["fkv"]
    for dx in range(1, xs):
        tx = across(dx)
        remote(pkv.at[pl.ds(tx * ZS, ZS)], xkv.at[dx - 1], 3, at(tx, z)).start()
    three = pl.ds(0, 3)
    arrive(2, fq.at[three])

    qa = r["qa"]
    qa[owned] = jnp.sum(fq[...], axis=0).astype(BF16)

    @pl.loop(0, near)
    def _(j):
        tx, tz = neighbour(j)
        remote(qa.at[owned], qa.at[owned], 4, at(tx, tz)).start()

    arrive(3, xkv)
    skv[...] = pkv[pl.ds(x * ZS, ZS)] + jnp.sum(xkv[...], axis=0)
    for i, dz in enumerate((2, 1, -1)):
        tz = lax.rem(z + dz + ZS, ZS)
        remote(skv.at[pl.ds(lax.rem(tz, 4) * 4, 4)], nkv.at[i], 5, at(x, tz)).start()

    query = qa[mine]
    row_ids = lax.broadcasted_iota(jnp.int32, (8, 1), 0)
    loads["lk"].wait()
    loads["lv"].wait()
    leaf_scores = jnp.zeros((8, leaf_max), F32)
    for h in range(heads):
        leaf_scores = jnp.where(row_ids == h, dot_t(query, r["lk"][h]), leaf_scores)
    leaf_on = r["leaf_mask"][...] > 0.0
    leaf_scores = jnp.where(leaf_on, leaf_scores * scale, NEGATIVE)
    leaf_m = jnp.max(leaf_scores, axis=1, keepdims=True)
    leaf_w = jnp.where(leaf_on, jnp.exp(leaf_scores - leaf_m), 0.0).astype(BF16)
    leaf_l = jnp.sum(leaf_w.astype(F32), axis=1, keepdims=True)
    leaf_n = jnp.zeros((8, head_size), F32)
    for h in range(heads):
        leaf_n = jnp.where(row_ids == h, dot(leaf_w, r["lv"][h]), leaf_n)

    arrive(5, nkv)
    tkv[...] = skv[pl.ds(lax.rem(z, 4) * 4, 4)] + jnp.sum(nkv[...], axis=0)
    for i, tz in enumerate(distant):
        remote(tkv.at[tz // 4], fkv.at[i], 6, at(x, tz)).start()
    loads["k"].wait()
    loads["v"].wait()
    arrive(4, qa.at[pl.ds(0, near * 4)])

    qf = r["qf"]
    qf[...] = qa[...].astype(F32)
    lanes = lax.broadcasted_iota(jnp.int32, (nodes, 128), 1)
    stat_m = jnp.full((nodes, 128), NEGATIVE, F32)
    stat_l = jnp.zeros((nodes, 128), F32)
    nb32, nb, st = r["nb32"], r["nb"], r["st"]
    for h in range(heads):
        qh = qf[:, h, :].astype(BF16)
        on = r["mask"][...] > 0.0
        scores = jnp.concatenate([dot_t(qh, r["k"][p, h]) for p in range(seg_dev)], axis=1)
        scores = jnp.where(on, scores * scale, NEGATIVE)
        top = jnp.max(scores, axis=1, keepdims=True)
        weights = jnp.where(on, jnp.exp(scores - top), 0.0).astype(BF16)
        total = jnp.sum(weights.astype(F32), axis=1, keepdims=True)
        summed = dot(weights[:, :seg], r["v"][0, h])
        for p in range(1, seg_dev):
            summed = summed + dot(weights[:, p * seg : (p + 1) * seg], r["v"][p, h])
        nb32[:, h, :] = summed
        stat_m = jnp.where(lanes == h, top, stat_m)
        stat_l = jnp.where(lanes == h, total, stat_l)
    nb32[:, heads, :] = jnp.zeros((nodes, head_size), F32)
    nb[...] = nb32[...].astype(BF16)
    st[:, 0, :] = stat_m
    st[:, 1, :] = stat_l

    xn, xst, fn, fs = r["xn"], r["xst"], r["fn"], r["fs"]

    @pl.loop(0, near)
    def _(j):
        tx, tz = neighbour(j)
        there = pl.ds((tx * 4 + lax.rem(tz, 4)) * 4, 4)
        remote(st.at[there], xst.at[j], 7, at(tx, tz)).start()
        remote(nb.at[there], xn.at[j], 8, at(tx, tz)).start()

    xst[near] = st[owned]
    xn[near] = nb[owned]
    diagonal = lax.broadcasted_iota(jnp.int32, (8, 128), 0) == lax.broadcasted_iota(
        jnp.int32, (8, 128), 1
    )

    def upright(row):
        spread = jnp.broadcast_to(row, (8, 128))
        return jnp.sum(jnp.where(diagonal, spread, 0.0), axis=1, keepdims=True)

    def flat(col, rest):
        spread = jnp.sum(jnp.where(diagonal, jnp.broadcast_to(col, (8, 128)), 0.0), axis=0, keepdims=True)
        return jnp.where(lax.broadcasted_iota(jnp.int32, (1, 128), 1) < 8, spread, rest)

    arrive(6, fkv)
    new = (tkv[turn] + jnp.sum(fkv[...], axis=0)).astype(BF16).astype(F32)
    own_m = jnp.sum(query.astype(F32) * new[:, :head_size], axis=1, keepdims=True) * scale
    extra_m = jnp.maximum(own_m, leaf_m)
    own_f, leaf_f = jnp.exp(own_m - extra_m), jnp.exp(leaf_m - extra_m)
    extra_l = own_f + leaf_f * leaf_l
    extra_n = own_f * new[:, head_size:] + leaf_f * leaf_n
    is_mine = lax.broadcasted_iota(jnp.int32, (4, 1), 0) == turn
    extra_ms = jnp.where(is_mine, flat(extra_m, NEGATIVE), NEGATIVE)
    extra_ls = jnp.where(is_mine, flat(extra_l, 0.0), 0.0)

    arrive(7, xst.at[pl.ds(0, near)])
    ms = xst[:, :, 0, :]
    top = jnp.maximum(jnp.max(ms, axis=0), extra_ms)
    factors = jnp.exp(ms - top[None])
    extra_f = jnp.where(is_mine, jnp.exp(extra_ms - top), 0.0)
    total = jnp.sum(factors * xst[:, :, 1, :], axis=0) + extra_f * extra_ls
    fs[turn, :, 0, :] = top
    fs[turn, :, 1, :] = total
    for tz in distant:
        remote(fs.at[turn], fs.at[turn], 9, at(x, tz)).start()
    arrive(8, xn.at[pl.ds(0, near)])
    for i in range(4):
        summed = upright(extra_f[i : i + 1]) * extra_n
        for s in range(near + 1):
            summed = summed + upright(factors[s, i : i + 1]) * xn[s, i].astype(F32)
        fn[turn, i] = summed.astype(BF16)
    for tz in distant:
        remote(fn.at[turn], fn.at[turn], 10, at(x, tz)).start()
    arrive(9, fs.at[three])
    ms = fs[:, :, 0, :]
    top = jnp.max(ms, axis=0)
    factors = jnp.exp(ms - top[None])
    total = jnp.sum(factors * fs[:, :, 1, :], axis=0)
    total = jnp.where(lax.broadcasted_iota(jnp.int32, (4, 128), 1) < heads, total, 1.0)
    factors = factors / total[None]
    factors = [[upright(factors[s, i : i + 1]) for s in range(4)] for i in range(4)]
    arrive(10, fn.at[three])

    aa = r["aa"]
    for i in range(4):
        attended = sum(factors[i][s] * fn[s, i].astype(F32) for s in range(4))
        aa[block * 4 + i] = attended.astype(BF16)

    @pl.loop(0, near)
    def _(j):
        tx, tz = neighbour(j)
        remote(aa.at[owned], aa.at[owned], 11, at(tx, tz)).start()

    loads["wo"].wait()
    arrive(11, aa.at[pl.ds(0, near * 4)])

    for n in range(nodes):
        qf[n] = aa[rho(n)].astype(F32)
    acc = jnp.zeros((nodes, out_width), F32)
    for h in range(heads):
        acc = acc + dot_t(qf[:, h, :].astype(BF16), r["wo"][:, h * head_size : (h + 1) * head_size])
    rows_out = nodes // heads_n
    os, orr = r["os"], r["orr"]
    os[:, :, pl.ds(0, out_width)] = acc.reshape(heads_n, rows_out, out_width)
    for dh in range(1, heads_n):
        th = lax.rem(hd + dh, heads_n)
        remote(os.at[th], orr.at[dh - 1], 12, {"nodes": me, "heads": th}).start()
    arrive(12, orr)
    result = os[hd] + jnp.sum(orr[...], axis=0)
    r["out"][...] = result[:, :out_width].astype(BF16)

    for sem, ref in sent:
        remote(ref, ref, sem, other).wait_send()


def on_device(
    hidden,
    norm_gain,
    qkv_weight,
    out_weight,
    prefix_keys,
    prefix_values,
    leaf_keys,
    leaf_values,
    piece_node,
    mid_parent,
    leaf_parent,
    leaf_len,
    sink_len,
    window_len,
):
    nodes = lax.axis_size("nodes")
    heads_n = lax.axis_size("heads")
    xs = nodes // ZS
    width, heads, triple = qkv_weight.shape
    head_size = triple // 3
    seg_dev, seg = prefix_keys.shape[:2]
    leaf_max = leaf_keys.shape[1]
    out_width = out_weight.shape[1]
    rows_out = nodes // heads_n
    dims = (nodes, heads_n, heads, head_size, width, seg_dev, seg, leaf_max, out_width)
    large = {
        "hidden_hbm": hidden,
        "gain_hbm": norm_gain[None, :],
        "pn_hbm": piece_node[None, :],
        "mp_hbm": mid_parent[None, :],
        "lp_hbm": leaf_parent[None, :],
        "ll_hbm": leaf_len[None, :],
        "sl_hbm": sink_len[None, :],
        "wl_hbm": window_len[None, :],
        "w_hbm": qkv_weight.transpose(1, 0, 2),
        "wo_hbm": out_weight.T,
        "k_hbm": prefix_keys.transpose(0, 2, 1, 3),
        "v_hbm": prefix_values.transpose(0, 2, 1, 3),
        "lk_hbm": leaf_keys[0].transpose(1, 0, 2),
        "lv_hbm": leaf_values[0].transpose(1, 0, 2),
    }
    vmem = pltpu.VMEM
    scratch = {n[:-4]: vmem(a.shape, a.dtype) for n, a in large.items()}
    scratch |= {
        "rows": vmem((nodes, 1, 128), F32),
        "cols": vmem((nodes, 1, 128), F32),
        "mask": vmem((nodes, seg_dev * seg), F32),
        "leaf_mask": vmem((8, leaf_max), F32),
        "pq": vmem((nodes, 8, head_size), F32),
        "nq": vmem((xs * 4 - 1, 4, 8, head_size), F32),
        "fq": vmem((4, 4, 8, head_size), F32),
        "pkv": vmem((nodes, 8, 2 * head_size), F32),
        "xkv": vmem((xs - 1, ZS, 8, 2 * head_size), F32),
        "skv": vmem((ZS, 8, 2 * head_size), F32),
        "nkv": vmem((3, 4, 8, 2 * head_size), F32),
        "tkv": vmem((4, 8, 2 * head_size), F32),
        "fkv": vmem((3, 8, 2 * head_size), F32),
        "qa": vmem((nodes, 8, head_size), BF16),
        "aa": vmem((nodes, 8, head_size), BF16),
        "qf": vmem((nodes, 8, head_size), F32),
        "nb32": vmem((nodes, 8, head_size), F32),
        "nb": vmem((nodes, 8, head_size), BF16),
        "xn": vmem((xs * 4, 4, 8, head_size), BF16),
        "st": vmem((nodes, 2, 128), F32),
        "xst": vmem((xs * 4, 4, 2, 128), F32),
        "fn": vmem((4, 4, 8, head_size), BF16),
        "fs": vmem((4, 4, 2, 128), F32),
        "os": vmem((heads_n, rows_out, 128), F32),
        "orr": vmem((heads_n - 1, rows_out, 128), F32),
        "load": pltpu.SemaphoreType.DMA((len(LOADED),)),
        "send": pltpu.SemaphoreType.DMA((13,)),
        "recv": pltpu.SemaphoreType.DMA((13,)),
    }
    names = list(large) + ["out"] + list(scratch)
    return pl.pallas_call(
        functools.partial(kernel, dims, names),
        out_shape=jax.ShapeDtypeStruct((rows_out, out_width), BF16),
        in_specs=[pl.BlockSpec(memory_space=pl.ANY)] * len(large),
        out_specs=pl.BlockSpec(memory_space=pltpu.VMEM),
        scratch_shapes=list(scratch.values()),
        compiler_params=pltpu.CompilerParams(
            collective_id=0, has_side_effects=True, vmem_limit_bytes=60 * 2**20
        ),
    )(*large.values())


def solution(mesh):
    return jax.shard_map(
        on_device,
        mesh=mesh,
        in_specs=(
            P("nodes", None),
            P(),
            P("nodes", "heads", None),
            P("heads", "nodes"),
            P("nodes", None, "heads", None),
            P("nodes", None, "heads", None),
            P("nodes", None, "heads", None),
            P("nodes", None, "heads", None),
            P(),
            P(),
            P(),
            P(),
            P(),
            P(),
        ),
        out_specs=P("heads", "nodes"),
        check_vma=False,
    )
```

time: 83.6 us -> 73.6 us (0.88)
  Pallas kernels: 82.1 us -> 72.2 us
    pallas_call x1, Pallas kernels: 82.1 us -> 72.2 us  [on_device(): pl.pallas_call(functools.partial(kernel, dims, names), out_shape=jax.Shap...]
where the time goes in v2:
time: 73.6 us; the launch traced here: 73.5 us
  Pallas kernels  72.2 us (98%)
  local copies, waits for them, and re-layouts  1.26 us (2%)
    pallas_call x1, Pallas kernels, on_device(): pl.pallas_call(functools.partial(kernel, dims, names), out_shape=jax.Shap...  72.2 us

profile of v2, /device:TPU:1, one launch (start us, length us, event | category | flops | bytes accessed | tf_op | source)
XLA Modules:
  0.0 73.5 jit_solution(1019269895762070593)
XLA Ops:
  0.0 72.2 %shard_map.136 = bf16[8,112]{1,0:T(8,128)(2,1)} custom-call(bf16[1,7168]{1,0:T(2,128)(2,1)} %refs_0_.1, f32[1,7168]{1,0:T(1,128)} %bitcast.23, s32[1,256]{1,0:T(1,128)} %bitcast.24, s32[1,32]{1,0:T(1,128)} %bitcast.25, s32[1,64]{1,0:T(1,128)} %bitcast.26, s32[1,64]{1,0:T(1,128)} %bitcast.27, s32[1,64]{1,0:T(1,128)} %bitcast.28, s32[1,64]{1,0:T(1,128)} %bitcast.29, ...), custom_call_target="tpu_custom_call" | custom-call | tf_op jit(solution)/shard_map/pallas_call | solution.py:443
  72.2 1.3 %copy.16 = bf16[8,112]{1,0:T(8,128)(2,1)} copy(bf16[8,112]{1,0:T(8,128)(2,1)} %shard_map.136) | data formatting | bytes 3584

commit v3 on v2

--- a/solution.py
+++ b/solution.py
@@ -249,8 +249,8 @@
     qf = r["qf"]
     qf[...] = qa[...].astype(F32)
     lanes = lax.broadcasted_iota(jnp.int32, (nodes, 128), 1)
-    stat_m = jnp.full((nodes, 128), NEGATIVE, F32)
-    stat_l = jnp.zeros((nodes, 128), F32)
+    base = 16 * (lax.broadcasted_iota(jnp.int32, (nodes, 128), 0) % 4)
+    stats = jnp.zeros((nodes, 128), F32)
     nb32, nb, st = r["nb32"], r["nb"], r["st"]
     for h in range(heads):
         qh = qf[:, h, :].astype(BF16)
@@ -264,35 +264,39 @@
         for p in range(1, seg_dev):
             summed = summed + dot(weights[:, p * seg : (p + 1) * seg], r["v"][p, h])
         nb32[:, h, :] = summed
-        stat_m = jnp.where(lanes == h, top, stat_m)
-        stat_l = jnp.where(lanes == h, total, stat_l)
+        stats = jnp.where(lanes == base + h, top, stats)
+        stats = jnp.where(lanes == base + (8 + h), total, stats)
     nb32[:, heads, :] = jnp.zeros((nodes, head_size), F32)
     nb[...] = nb32[...].astype(BF16)
-    st[:, 0, :] = stat_m
-    st[:, 1, :] = stat_l
+    r["st32"][...] = stats
+    st[:, 0, :] = sum(r["st32"][pl.ds(i, nodes // 4, stride=4), :] for i in range(4))
 
     xn, xst, fn, fs = r["xn"], r["xst"], r["fn"], r["fs"]
 
     @pl.loop(0, near)
     def _(j):
         tx, tz = neighbour(j)
-        there = pl.ds((tx * 4 + lax.rem(tz, 4)) * 4, 4)
+        there = tx * 4 + lax.rem(tz, 4)
         remote(st.at[there], xst.at[j], 7, at(tx, tz)).start()
-        remote(nb.at[there], xn.at[j], 8, at(tx, tz)).start()
-
-    xst[near] = st[owned]
+        remote(nb.at[pl.ds(there * 4, 4)], xn.at[j], 8, at(tx, tz)).start()
+
+    xst[near] = st[block]
     xn[near] = nb[owned]
-    diagonal = lax.broadcasted_iota(jnp.int32, (8, 128), 0) == lax.broadcasted_iota(
-        jnp.int32, (8, 128), 1
-    )
-
-    def upright(row):
+    upper = lax.broadcasted_iota(jnp.int32, (8, 128), 0)
+    lane8 = lax.broadcasted_iota(jnp.int32, (8, 128), 1)
+    lane = lax.broadcasted_iota(jnp.int32, (1, 128), 1)
+    maximum_lane = lane % 16 < 8
+
+    def upright(row, i):
         spread = jnp.broadcast_to(row, (8, 128))
-        return jnp.sum(jnp.where(diagonal, spread, 0.0), axis=1, keepdims=True)
-
-    def flat(col, rest):
-        spread = jnp.sum(jnp.where(diagonal, jnp.broadcast_to(col, (8, 128)), 0.0), axis=0, keepdims=True)
-        return jnp.where(lax.broadcasted_iota(jnp.int32, (1, 128), 1) < 8, spread, rest)
+        return jnp.sum(jnp.where(lane8 == upper + 16 * i, spread, 0.0), axis=1, keepdims=True)
+
+    def flat(col, at_lane):
+        spread = jnp.broadcast_to(col, (8, 128))
+        return jnp.sum(jnp.where(lane8 == upper + at_lane, spread, 0.0), axis=0, keepdims=True)
+
+    def onward(factors):
+        return pltpu.roll(factors, 8, 1)
 
     arrive(6, fkv)
     new = (tkv[turn] + jnp.sum(fkv[...], axis=0)).astype(BF16).astype(F32)
@@ -301,36 +305,35 @@
     own_f, leaf_f = jnp.exp(own_m - extra_m), jnp.exp(leaf_m - extra_m)
     extra_l = own_f + leaf_f * leaf_l
     extra_n = own_f * new[:, head_size:] + leaf_f * leaf_n
-    is_mine = lax.broadcasted_iota(jnp.int32, (4, 1), 0) == turn
-    extra_ms = jnp.where(is_mine, flat(extra_m, NEGATIVE), NEGATIVE)
-    extra_ls = jnp.where(is_mine, flat(extra_l, 0.0), 0.0)
+    my_maxima = (lane >= 16 * turn) & (lane < 16 * turn + 8)
+    extra = flat(extra_m, 16 * turn) + flat(extra_l, 16 * turn + 8)
+    extra = jnp.where(maximum_lane & ~my_maxima, NEGATIVE, extra)
 
     arrive(7, xst.at[pl.ds(0, near)])
-    ms = xst[:, :, 0, :]
-    top = jnp.maximum(jnp.max(ms, axis=0), extra_ms)
-    factors = jnp.exp(ms - top[None])
-    extra_f = jnp.where(is_mine, jnp.exp(extra_ms - top), 0.0)
-    total = jnp.sum(factors * xst[:, :, 1, :], axis=0) + extra_f * extra_ls
-    fs[turn, :, 0, :] = top
-    fs[turn, :, 1, :] = total
+    stats = xst[:, 0, :]
+    top = jnp.maximum(jnp.max(stats, axis=0, keepdims=True), extra)
+    factors = jnp.exp(stats - top)
+    extra_f = jnp.where(my_maxima, jnp.exp(extra - top), 0.0)
+    total = jnp.sum(onward(factors) * stats, axis=0, keepdims=True) + onward(extra_f) * extra
+    fs[turn] = jnp.where(maximum_lane, top, total)
     for tz in distant:
         remote(fs.at[turn], fs.at[turn], 9, at(x, tz)).start()
     arrive(8, xn.at[pl.ds(0, near)])
     for i in range(4):
-        summed = upright(extra_f[i : i + 1]) * extra_n
+        summed = upright(extra_f, i) * extra_n
         for s in range(near + 1):
-            summed = summed + upright(factors[s, i : i + 1]) * xn[s, i].astype(F32)
+            summed = summed + upright(factors[s : s + 1], i) * xn[s, i].astype(F32)
         fn[turn, i] = summed.astype(BF16)
-    for tz in distant:
-        remote(fn.at[turn], fn.at[turn], 10, at(x, tz)).start()
+        for tz in distant:
+            remote(fn.at[turn, i], fn.at[turn, i], 10, at(x, tz)).start()
     arrive(9, fs.at[three])
-    ms = fs[:, :, 0, :]
-    top = jnp.max(ms, axis=0)
-    factors = jnp.exp(ms - top[None])
-    total = jnp.sum(factors * fs[:, :, 1, :], axis=0)
-    total = jnp.where(lax.broadcasted_iota(jnp.int32, (4, 128), 1) < heads, total, 1.0)
-    factors = factors / total[None]
-    factors = [[upright(factors[s, i : i + 1]) for s in range(4)] for i in range(4)]
+    stats = fs[:, 0, :]
+    top = jnp.max(stats, axis=0, keepdims=True)
+    factors = jnp.exp(stats - top)
+    total = jnp.sum(onward(factors) * stats, axis=0, keepdims=True)
+    total = pltpu.roll(total, 120, 1)
+    factors = factors / jnp.where(maximum_lane & (lane < 64), total, 1.0)
+    factors = [[upright(factors[s : s + 1], i) for s in range(4)] for i in range(4)]
     arrive(10, fn.at[three])
 
     aa = r["aa"]
@@ -429,10 +432,11 @@
         "nb32": vmem((nodes, 8, head_size), F32),
         "nb": vmem((nodes, 8, head_size), BF16),
         "xn": vmem((xs * 4, 4, 8, head_size), BF16),
-        "st": vmem((nodes, 2, 128), F32),
-        "xst": vmem((xs * 4, 4, 2, 128), F32),
+        "st32": vmem((nodes, 128), F32),
+        "st": vmem((nodes // 4, 1, 128), F32),
+        "xst": vmem((xs * 4, 1, 128), F32),
         "fn": vmem((4, 4, 8, head_size), BF16),
-        "fs": vmem((4, 4, 2, 128), F32),
+        "fs": vmem((4, 1, 128), F32),
         "os": vmem((heads_n, rows_out, 128), F32),
         "orr": vmem((heads_n - 1, rows_out, 128), F32),
         "load": pltpu.SemaphoreType.DMA((len(LOADED),)),

time: 73.6 us -> 72.4 us (0.984)
  Pallas kernels: 72.2 us -> 71 us
    pallas_call x1, Pallas kernels: 72.2 us -> 71 us  [on_device(): pl.pallas_call(functools.partial(kernel, dims, names), out_shape=jax.Shap...]
where the time goes in v3:
time: 72.4 us; the launch traced here: 72.3 us
  Pallas kernels  71 us (98%)
  local copies, waits for them, and re-layouts  1.26 us (2%)
    pallas_call x1, Pallas kernels, on_device(): pl.pallas_call(functools.partial(kernel, dims, names), out_shape=jax.Shap...  71 us

profile of v3, /device:TPU:1, one launch (start us, length us, event | category | flops | bytes accessed | tf_op | source)
XLA Modules:
  0.0 72.3 jit_solution(7411472392787417855)
XLA Ops:
  0.0 71.0 %shard_map.136 = bf16[8,112]{1,0:T(8,128)(2,1)} custom-call(bf16[1,7168]{1,0:T(2,128)(2,1)} %refs_0_.1, f32[1,7168]{1,0:T(1,128)} %bitcast.23, s32[1,256]{1,0:T(1,128)} %bitcast.24, s32[1,32]{1,0:T(1,128)} %bitcast.25, s32[1,64]{1,0:T(1,128)} %bitcast.26, s32[1,64]{1,0:T(1,128)} %bitcast.27, s32[1,64]{1,0:T(1,128)} %bitcast.28, s32[1,64]{1,0:T(1,128)} %bitcast.29, ...), custom_call_target="tpu_custom_call" | custom-call | tf_op jit(solution)/shard_map/pallas_call | solution.py:447
  71.0 1.3 %copy.16 = bf16[8,112]{1,0:T(8,128)(2,1)} copy(bf16[8,112]{1,0:T(8,128)(2,1)} %shard_map.136) | data formatting | bytes 3584

commit v4 on v3

v4 whole, which is shorter than its diff:
```python
import functools
import math

import jax
import jax.numpy as jnp
from jax import lax
from jax.experimental import pallas as pl
from jax.experimental.pallas import tpu as pltpu
from jax.sharding import PartitionSpec as P

MESH = pl.DeviceIdType.MESH
F32 = jnp.float32
BF16 = jnp.bfloat16
ROOTS = 4
EPSILON = 1e-05
NEGATIVE = -1e30
LOADED = ("hidden", "gain", "pn", "mp", "lp", "ll", "sl", "wl", "w", "k", "v", "lk", "lv", "wo")
SEM = {
    n: i
    for i, n in enumerate(
        ("rows", "twin", "nq0", "nq1", "fq", "qa0", "qa1", "xkv0", "xkv1", "nkv", "fkv", "leaf")
        + ("xst0", "xst1", "xn0", "xn1", "fs", "fn0", "fn1", "aa0", "aa1", "out")
    )
}
ZS = 16


def rho(n):
    z = lax.rem(n, ZS) if not isinstance(n, int) else n % ZS
    return n - z + (z % 4) * 4 + z // 4


def column(row):
    n = row.shape[1]
    i = lax.broadcasted_iota(jnp.int32, (n, n), 0)
    here = (i // ZS) * ZS + (i % 4) * 4 + (i % ZS) // 4 == lax.broadcasted_iota(jnp.int32, (n, n), 1)
    return jnp.sum(jnp.where(here, jnp.broadcast_to(row, (n, n)), 0.0), axis=1, keepdims=True)


def dot_t(a, b):
    return lax.dot_general(a, b, (((1,), (1,)), ((), ())), preferred_element_type=F32)


def dot(a, b):
    return jnp.dot(a, b, preferred_element_type=F32)


def kernel(dims, names, *refs):
    nodes, heads_n, heads, head_size, width, seg_dev, seg, leaf_max, out_width = dims
    r = dict(zip(names, refs, strict=True))
    xs = nodes // ZS
    me = lax.axis_index("nodes")
    hd = lax.axis_index("heads")
    x, z = me // ZS, lax.rem(me, ZS)
    core = lax.rem(hd, 2)
    hub, low, twin = hd + 1 - core, hd - core, hd + 1 - 2 * core
    mine, block, turn = rho(me), x * 4 + lax.rem(z, 4), z // 4
    scale = 1.0 / math.sqrt(head_size)
    near = xs * 4 - 1
    owned = pl.ds(block * 4, 4)
    fifteen, three = pl.ds(0, near), pl.ds(0, 3)

    def at(tx, tz, th):
        return {"nodes": tx * ZS + tz, "heads": th}

    def far(j):
        half = (j + 1) // 2
        return lax.rem(z + ZS // 2 + half * (1 - 2 * lax.rem(j, 2)), ZS)

    def across(j):
        return lax.rem(x + j, xs)

    def offsets_of(j):
        i, k = lax.rem(j, 4), j // 4
        return 2 + ((i + 1) // 2) * (1 - 2 * lax.rem(i, 2)), 2 - k - k // 2 + 2 * (k // 3)

    def neighbour(j):
        dx, dz = offsets_of(j)
        return lax.rem(x + dx, xs), lax.rem(z + dz + ZS, ZS)

    def copy(src, dst, sem, target):
        return pltpu.make_async_remote_copy(
            src_ref=src,
            dst_ref=dst,
            send_sem=r["send"].at[sem],
            recv_sem=r["recv"].at[sem],
            device_id=target,
            device_id_type=MESH,
        )

    def remote(src, dst, sem, target):
        copy(src, dst, SEM[sem] if isinstance(sem, str) else sem, target).start()

    def arrive(sem, ref):
        copy(ref, ref, SEM[sem], at(x, z, twin)).wait_recv()

    def left(sem, ref):
        copy(ref, ref, SEM[sem], at(x, z, twin)).wait_send()

    on_hub, on_low = pl.when(core == 1), pl.when(core == 0)
    distant = [lax.rem(z + 4 * d, ZS) for d in (2, 1, 3)]

    loads = {
        n: pltpu.make_async_copy(r[n + "_hbm"], r[n], r["load"].at[i])
        for i, n in enumerate(LOADED)
    }
    loads["hidden"].start()
    loads["gain"].start()
    barrier = pltpu.get_barrier_semaphore()

    def tell(target):
        pl.semaphore_signal(barrier, inc=1, device_id=target, device_id_type=MESH)

    @on_hub
    def _():
        @pl.loop(0, ZS - 1)
        def _(j):
            for dx in (2, 1, 3, 0):
                tell(at(across(dx), far(j), hd))

        for dx in range(1, xs):
            tell(at(across(dx), z, hd))

    @pl.loop(0, near)
    def _(j):
        dx, dz = offsets_of(j)
        tell(at(lax.rem(x - dx + 2 * xs, xs), lax.rem(z - dz + ZS, ZS), twin))

    for dh in range(1, heads_n):
        tell({"nodes": me, "heads": lax.rem(hd + dh, heads_n)})

    for n in LOADED[2:]:
        loads[n].start()
    loads["hidden"].wait()
    loads["gain"].wait()

    rows, cols = r["rows"], r["cols"]

    @on_hub
    def _():
        values = r["hidden"][...].astype(F32)
        features = values.shape[1]
        mean = jnp.sum(values, axis=1, keepdims=True) * (1.0 / features)
        centered = values - mean
        variance = jnp.sum(centered * centered, axis=1, keepdims=True) * (1.0 / features)
        normed = centered * lax.rsqrt(variance + EPSILON) * r["gain"][...]
        normed = normed.astype(BF16).astype(F32)
        for n in range(nodes):
            rows[n, :, pl.ds(0, width)] = normed[:, n * width : (n + 1) * width]

        pl.semaphore_wait(barrier, nodes - 1 + near + heads_n - 1)

        @pl.loop(0, ZS - 1)
        def _(j):
            tz = far(j)
            for dx in (2, 1, 3, 0):
                tx = across(dx)
                remote(rows.at[tx * ZS + tz], cols.at[mine], "rows", at(tx, tz, hd))

        for dx in range(1, xs):
            tx = across(dx)
            remote(rows.at[tx * ZS + z], cols.at[mine], "rows", at(tx, z, hd))
        cols[mine] = rows[me]

    @on_low
    def _():
        pl.semaphore_wait(barrier, near + heads_n - 1)

    for n in ("pn", "mp", "lp", "ll", "sl", "wl"):
        loads[n].wait()
    pn = r["pn"][...].astype(F32)
    pieces = pn.shape[1]
    mids = r["mp"].shape[1]
    parent = column(r["lp"][...].astype(F32))
    leaf_len = column(r["ll"][...].astype(F32))
    sink = column(r["sl"][...].astype(F32))
    window = column(r["wl"][...].astype(F32))
    mid_ids = lax.broadcasted_iota(jnp.int32, (nodes, mids), 1).astype(F32)
    mp = jnp.broadcast_to(r["mp"][...].astype(F32), (nodes, mids))
    root_node = jnp.sum(jnp.where(mid_ids == parent, mp, 0.0), axis=1, keepdims=True)
    mid_node = parent + float(ROOTS)
    pn_all = jnp.broadcast_to(pn, (nodes, pieces))
    root_len = float(seg) * jnp.sum(jnp.where(pn_all == root_node, 1.0, 0.0), axis=1, keepdims=True)
    mid_len = float(seg) * jnp.sum(jnp.where(pn_all == mid_node, 1.0, 0.0), axis=1, keepdims=True)
    finish = root_len + mid_len + leaf_len
    since = finish - window
    piece_ids = lax.broadcasted_iota(jnp.int32, (1, pieces), 1)
    offsets = lax.broadcasted_iota(jnp.int32, (nodes, seg), 1).astype(F32)
    for p in range(seg_dev):
        here = me * seg_dev + p
        node = jnp.sum(jnp.where(piece_ids == here, pn, 0.0), axis=1, keepdims=True)
        same = (pn == node) & (piece_ids < here)
        rank = jnp.sum(jnp.where(same, 1.0, 0.0), axis=1, keepdims=True)
        at_mid = mid_node == node
        start = jnp.where(at_mid, root_len, 0.0) + rank * float(seg)
        position = offsets + start
        visible = ((position < sink) | (position >= since)) & (at_mid | (root_node == node))
        r["mask"][:, p * seg : (p + 1) * seg] = jnp.where(visible, 1.0, 0.0)
    my_row = lax.broadcasted_iota(jnp.int32, (nodes, 1), 0) == mine

    def mine_of(values):
        return jnp.sum(jnp.where(my_row, values, 0.0), axis=0, keepdims=True)

    my_finish, my_leaf, my_sink = mine_of(finish), mine_of(leaf_len), mine_of(sink)
    my_low = mine_of(since)
    leaf_offsets = lax.broadcasted_iota(jnp.int32, (8, leaf_max), 1).astype(F32)
    leaf_position = leaf_offsets + (my_finish - my_leaf)
    leaf_visible = ((leaf_position < my_sink) | (leaf_position >= my_low)) & (leaf_offsets < my_leaf)
    r["leaf_mask"][...] = jnp.where(leaf_visible, 1.0, 0.0)

    pq, pkv = r["pq"], r["pkv"]
    pq[:, heads, :] = jnp.zeros((nodes, head_size), F32)
    pkv[:, heads, :] = jnp.zeros((nodes, 2 * head_size), F32)
    loads["w"].wait()

    @on_hub
    def _():
        arrive("rows", cols.at[pl.ds(0, nodes - 1)])
        remote(cols, cols, "twin", at(x, z, low))

    @on_low
    def _():
        arrive("twin", cols)

    lhs = cols[:, 0, :][:, :width].astype(BF16)
    for h in range(heads):
        pq[:, h, :] = dot(lhs, r["w"][h, :, pl.ds(0, head_size)])
    nq, fq = r["nq"], r["fq"]

    @pl.loop(0, near)
    def _(j):
        tx, tz = neighbour(j)
        src = pq.at[pl.ds((tx * 4 + lax.rem(tz, 4)) * 4, 4)]
        remote(src, nq.at[core, j], SEM["nq0"] + core, at(tx, tz, hub))

    @on_low
    def _():
        remote(pq.at[owned], nq.at[0, near], "nq0", at(x, z, hub))

    for h in range(heads):
        pkv[:, h, :] = dot(lhs, r["w"][h, :, pl.ds(head_size, 2 * head_size)])

    @on_hub
    def _():
        nq[1, near] = pq[owned]
        arrive("nq1", nq.at[1, fifteen])
        fq[turn, 1] = jnp.sum(nq[1], axis=0)
        arrive("nq0", nq.at[0])
        fq[turn, 0] = jnp.sum(nq[0], axis=0)
        for tz in distant:
            remote(fq.at[turn], fq.at[turn], "fq", at(x, tz, hd))
        pl.semaphore_signal(r["go"], inc=1, device_id=at(x, z, low), device_id_type=MESH)

    @on_low
    def _():
        pl.semaphore_wait(r["go"], 1)

    xkv, skv, nkv, tkv, fkv = r["xkv"], r["skv"], r["nkv"], r["tkv"], r["fkv"]
    row = pl.ds(x * ZS, ZS)
    for dx in range(1, xs):
        tx = across(dx)
        remote(pkv.at[pl.ds(tx * ZS, ZS)], xkv.at[core, dx - 1], SEM["xkv0"] + core, at(tx, z, hub))

    @on_low
    def _():
        remote(pkv.at[row], xkv.at[0, xs - 1], "xkv0", at(x, z, hub))

    qa, q0 = r["qa"], r["q0"]
    row_ids = lax.broadcasted_iota(jnp.int32, (8, 1), 0)
    leaf = r["leaf"]

    def leaf_part(at_core):
        query = qa[mine]
        scores = jnp.zeros((8, leaf_max), F32)
        for h in range(heads):
            scores = jnp.where(row_ids == h, dot_t(query, r["lk"][h]), scores)
        on = r["leaf_mask"][...] > 0.0
        scores = jnp.where(on, scores * scale, NEGATIVE)
        top = jnp.max(scores, axis=1, keepdims=True)
        weights = jnp.where(on, jnp.exp(scores - top), 0.0).astype(BF16)
        summed = jnp.zeros((8, head_size), F32)
        for h in range(heads):
            summed = jnp.where(row_ids == h, dot(weights, r["lv"][h]), summed)
        total = jnp.sum(weights.astype(F32), axis=1, keepdims=True)
        leaf[at_core, 0] = jnp.broadcast_to(top, (8, head_size))
        leaf[at_core, 1] = jnp.broadcast_to(total, (8, head_size))
        leaf[at_core, 2] = summed

    for n in ("lk", "lv", "k", "v"):
        loads[n].wait()

    @on_hub
    def _():
        xkv[1, xs - 1] = pkv[row]
        arrive("fq", fq.at[three])

        q0[...] = (fq[0, 0] + fq[1, 0] + fq[2, 0] + fq[3, 0]).astype(BF16)
        qa[owned] = (fq[0, 1] + fq[1, 1] + fq[2, 1] + fq[3, 1]).astype(BF16)

        @pl.loop(0, near)
        def _(j):
            tx, tz = neighbour(j)
            remote(q0, qa.at[owned], "qa0", at(tx, tz, low))
            remote(qa.at[owned], qa.at[owned], "qa1", at(tx, tz, hd))

        remote(q0, qa.at[owned], "qa0", at(x, z, low))
        arrive("xkv1", xkv.at[1, three])
        arrive("xkv0", xkv.at[0])
        for p in range(2):
            skv[:, p] = jnp.sum(xkv[p], axis=0)
        for i, dz in enumerate((2, 1, -1)):
            tz = lax.rem(z + dz + ZS, ZS)
            remote(skv.at[pl.ds(lax.rem(tz, 4) * 4, 4)], nkv.at[i], "nkv", at(x, tz, hd))
        leaf_part(1)
        arrive("nkv", nkv)
        tkv[...] = skv[pl.ds(lax.rem(z, 4) * 4, 4)] + jnp.sum(nkv[...], axis=0)
        for i, tz in enumerate(distant):
            remote(tkv.at[tz // 4], fkv.at[i], "fkv", at(x, tz, hd))
        arrive("qa1", qa.at[pl.ds(0, near * 4)])

    @on_low
    def _():
        arrive("qa0", qa)

    qf = r["qf"]
    qf[...] = qa[...].astype(F32)
    lanes = lax.broadcasted_iota(jnp.int32, (nodes, 128), 1)
    base = 16 * (lax.broadcasted_iota(jnp.int32, (nodes, 128), 0) % 4)
    stats = jnp.zeros((nodes, 128), F32)
    nb32, nb, st = r["nb32"], r["nb"], r["st"]
    for h in range(heads):
        qh = qf[:, h, :].astype(BF16)
        on = r["mask"][...] > 0.0
        scores = jnp.concatenate([dot_t(qh, r["k"][p, h]) for p in range(seg_dev)], axis=1)
        scores = jnp.where(on, scores * scale, NEGATIVE)
        top = jnp.max(scores, axis=1, keepdims=True)
        weights = jnp.where(on, jnp.exp(scores - top), 0.0).astype(BF16)
        total = jnp.sum(weights.astype(F32), axis=1, keepdims=True)
        summed = dot(weights[:, :seg], r["v"][0, h])
        for p in range(1, seg_dev):
            summed = summed + dot(weights[:, p * seg : (p + 1) * seg], r["v"][p, h])
        nb32[:, h, :] = summed
        stats = jnp.where(lanes == base + h, top, stats)
        stats = jnp.where(lanes == base + (8 + h), total, stats)
    nb32[:, heads, :] = jnp.zeros((nodes, head_size), F32)
    nb[...] = nb32[...].astype(BF16)
    r["st32"][...] = stats
    st[:, 0, :] = sum(r["st32"][pl.ds(i, nodes // 4, stride=4), :] for i in range(4))

    xn, xst, fn, fs = r["xn"], r["xst"], r["fn"], r["fs"]

    @pl.loop(0, near)
    def _(j):
        tx, tz = neighbour(j)
        there = tx * 4 + lax.rem(tz, 4)
        remote(st.at[there], xst.at[core, j], SEM["xst0"] + core, at(tx, tz, hub))
        remote(nb.at[pl.ds(there * 4, 4)], xn.at[core, j], SEM["xn0"] + core, at(tx, tz, hub))

    @on_low
    def _():
        remote(st.at[block], xst.at[0, near], "xst0", at(x, z, hub))
        remote(nb.at[owned], xn.at[0, near], "xn0", at(x, z, hub))
        leaf_part(0)
        remote(leaf.at[0], leaf.at[0], "leaf", at(x, z, hub))

    aa, a0 = r["aa"], r["a0"]
    upper = lax.broadcasted_iota(jnp.int32, (8, 128), 0)
    lane8 = lax.broadcasted_iota(jnp.int32, (8, 128), 1)
    lane = lax.broadcasted_iota(jnp.int32, (1, 128), 1)
    maximum_lane = lane % 16 < 8
    my_maxima = (lane >= 16 * turn) & (lane < 16 * turn + 8)

    def upright(row, i):
        spread = jnp.broadcast_to(row, (8, 128))
        return jnp.sum(jnp.where(lane8 == upper + 16 * i, spread, 0.0), axis=1, keepdims=True)

    def flat(col, at_lane):
        spread = jnp.broadcast_to(col, (8, 128))
        return jnp.sum(jnp.where(lane8 == upper + at_lane, spread, 0.0), axis=0, keepdims=True)

    def onward(factors):
        return pltpu.roll(factors, 8, 1)

    def extra_of(p):
        query = qa[mine] if p else q0[turn]
        new = tkv[turn, p] + fkv[0, p] + fkv[1, p] + fkv[2, p]
        new = new.astype(BF16).astype(F32)
        own_m = jnp.sum(query.astype(F32) * new[:, :head_size], axis=1, keepdims=True) * scale
        leaf_m, leaf_l = leaf[p, 0][:, :1], leaf[p, 1][:, :1]
        top = jnp.maximum(own_m, leaf_m)
        own_f, leaf_f = jnp.exp(own_m - top), jnp.exp(leaf_m - top)
        total = own_f + leaf_f * leaf_l
        extra = flat(top, 16 * turn) + flat(total, 16 * turn + 8)
        extra = jnp.where(maximum_lane & ~my_maxima, NEGATIVE, extra)
        return extra, own_f * new[:, head_size:] + leaf_f * leaf[p, 2]

    @on_hub
    def _():
        xst[1, near] = st[block]
        xn[1, near] = nb[owned]
        arrive("fkv", fkv)
        extras = {1: extra_of(1)}
        factors, extra_f = {}, {}
        for p in (1, 0):
            if p:
                arrive("xst1", xst.at[1, fifteen])
            else:
                arrive("leaf", leaf.at[0])
                extras[0] = extra_of(0)
                arrive("xst0", xst.at[0])
            stats, extra = xst[p, :, 0, :], extras[p][0]
            top = jnp.maximum(jnp.max(stats, axis=0, keepdims=True), extra)
            factors[p] = jnp.exp(stats - top)
            extra_f[p] = jnp.where(my_maxima, jnp.exp(extra - top), 0.0)
            total = jnp.sum(onward(factors[p]) * stats, axis=0, keepdims=True)
            total = total + onward(extra_f[p]) * extra
            fs[turn, p] = jnp.where(maximum_lane, top, total)
        for tz in distant:
            remote(fs.at[turn], fs.at[turn], "fs", at(x, tz, hd))
        for p in (1, 0):
            if p:
                arrive("xn1", xn.at[1, fifteen])
            else:
                arrive("xn0", xn.at[0])
            for i in range(4):
                summed = upright(extra_f[p], i) * extras[p][1]
                for s in range(near + 1):
                    summed = summed + upright(factors[p][s : s + 1], i) * xn[p, s, i].astype(F32)
                fn[turn, p, i] = summed.astype(BF16)
            for tz in distant:
                remote(fn.at[turn, p], fn.at[turn, p], "fn1" if p else "fn0", at(x, tz, hd))
        arrive("fs", fs.at[three])
        for p in (0, 1):
            stats = fs[:, p, 0, :]
            top = jnp.max(stats, axis=0, keepdims=True)
            f = jnp.exp(stats - top)
            total = pltpu.roll(jnp.sum(onward(f) * stats, axis=0, keepdims=True), 120, 1)
            f = f / jnp.where(maximum_lane & (lane < 64), total, 1.0)
            factors[p] = [[upright(f[s : s + 1], i) for s in range(4)] for i in range(4)]
        arrive("fn1", fn.at[three, 1])
        arrive("fn0", fn.at[three, 0])

        for p in (0, 1):
            for i in range(4):
                attended = sum(factors[p][i][s] * fn[s, p, i].astype(F32) for s in range(4))
                if p:
                    aa[block * 4 + i] = attended.astype(BF16)
                else:
                    a0[i] = attended.astype(BF16)

        @pl.loop(0, near)
        def _(j):
            tx, tz = neighbour(j)
            remote(a0, aa.at[owned], "aa0", at(tx, tz, low))
            remote(aa.at[owned], aa.at[owned], "aa1", at(tx, tz, hd))

        remote(a0, aa.at[owned], "aa0", at(x, z, low))

    loads["wo"].wait()

    @on_hub
    def _():
        arrive("aa1", aa.at[pl.ds(0, near * 4)])

    @on_low
    def _():
        arrive("aa0", aa)

    for n in range(nodes):
        qf[n] = aa[rho(n)].astype(F32)
    acc = jnp.zeros((nodes, out_width), F32)
    for h in range(heads):
        acc = acc + dot_t(qf[:, h, :].astype(BF16), r["wo"][:, h * head_size : (h + 1) * head_size])
    rows_out = nodes // heads_n
    os, orr = r["os"], r["orr"]
    os[:, :, pl.ds(0, out_width)] = acc.reshape(heads_n, rows_out, out_width)
    for dh in (4, 3, 5, 2, 6, 1, 7):
        th = lax.rem(hd + dh, heads_n)
        remote(os.at[th], orr.at[dh - 1], "out", {"nodes": me, "heads": th})
    arrive("out", orr)
    result = os[hd] + jnp.sum(orr[...], axis=0)
    r["out"][...] = result[:, :out_width].astype(BF16)

    left("out", orr)

    @on_low
    def _():
        left("nq0", nq.at[0])
        left("xkv0", xkv.at[0])
        left("leaf", leaf.at[0])
        left("xst0", xst.at[0])
        left("xn0", xn.at[0])

    @on_hub
    def _():
        left("rows", cols.at[pl.ds(0, nodes - 1)])
        left("twin", cols)
        left("nq1", nq.at[1, fifteen])
        left("fq", fq.at[three])
        left("qa0", qa)
        left("qa1", qa.at[pl.ds(0, near * 4)])
        left("xkv1", xkv.at[1, three])
        left("nkv", nkv)
        left("fkv", fkv)
        left("xst1", xst.at[1, fifteen])
        left("xn1", xn.at[1, fifteen])
        left("fs", fs.at[three])
        left("fn0", fn.at[three, 0])
        left("fn1", fn.at[three, 1])
        left("aa0", aa)
        left("aa1", aa.at[pl.ds(0, near * 4)])


def on_device(
    hidden,
    norm_gain,
    qkv_weight,
    out_weight,
    prefix_keys,
    prefix_values,
    leaf_keys,
    leaf_values,
    piece_node,
    mid_parent,
    leaf_parent,
    leaf_len,
    sink_len,
    window_len,
):
    nodes = lax.axis_size("nodes")
    heads_n = lax.axis_size("heads")
    xs = nodes // ZS
    width, heads, triple = qkv_weight.shape
    head_size = triple // 3
    seg_dev, seg = prefix_keys.shape[:2]
    leaf_max = leaf_keys.shape[1]
    out_width = out_weight.shape[1]
    rows_out = nodes // heads_n
    dims = (nodes, heads_n, heads, head_size, width, seg_dev, seg, leaf_max, out_width)
    large = {
        "hidden_hbm": hidden,
        "gain_hbm": norm_gain[None, :],
        "pn_hbm": piece_node[None, :],
        "mp_hbm": mid_parent[None, :],
        "lp_hbm": leaf_parent[None, :],
        "ll_hbm": leaf_len[None, :],
        "sl_hbm": sink_len[None, :],
        "wl_hbm": window_len[None, :],
        "w_hbm": qkv_weight.transpose(1, 0, 2),
        "wo_hbm": out_weight.T,
        "k_hbm": prefix_keys.transpose(0, 2, 1, 3),
        "v_hbm": prefix_values.transpose(0, 2, 1, 3),
        "lk_hbm": leaf_keys[0].transpose(1, 0, 2),
        "lv_hbm": leaf_values[0].transpose(1, 0, 2),
    }
    vmem = pltpu.VMEM
    scratch = {n[:-4]: vmem(a.shape, a.dtype) for n, a in large.items()}
    scratch |= {
        "rows": vmem((nodes, 1, 128), F32),
        "cols": vmem((nodes, 1, 128), F32),
        "mask": vmem((nodes, seg_dev * seg), F32),
        "leaf_mask": vmem((8, leaf_max), F32),
        "pq": vmem((nodes, 8, head_size), F32),
        "nq": vmem((2, xs * 4, 4, 8, head_size), F32),
        "fq": vmem((4, 2, 4, 8, head_size), F32),
        "pkv": vmem((nodes, 8, 2 * head_size), F32),
        "xkv": vmem((2, xs, ZS, 8, 2 * head_size), F32),
        "skv": vmem((ZS, 2, 8, 2 * head_size), F32),
        "nkv": vmem((3, 4, 2, 8, 2 * head_size), F32),
        "tkv": vmem((4, 2, 8, 2 * head_size), F32),
        "fkv": vmem((3, 2, 8, 2 * head_size), F32),
        "q0": vmem((4, 8, head_size), BF16),
        "a0": vmem((4, 8, head_size), BF16),
        "leaf": vmem((2, 3, 8, head_size), F32),
        "qa": vmem((nodes, 8, head_size), BF16),
        "aa": vmem((nodes, 8, head_size), BF16),
        "qf": vmem((nodes, 8, head_size), F32),
        "nb32": vmem((nodes, 8, head_size), F32),
        "nb": vmem((nodes, 8, head_size), BF16),
        "xn": vmem((2, xs * 4, 4, 8, head_size), BF16),
        "st32": vmem((nodes, 128), F32),
        "st": vmem((nodes // 4, 1, 128), F32),
        "xst": vmem((2, xs * 4, 1, 128), F32),
        "fn": vmem((4, 2, 4, 8, head_size), BF16),
        "fs": vmem((4, 2, 1, 128), F32),
        "os": vmem((heads_n, rows_out, 128), F32),
        "orr": vmem((heads_n - 1, rows_out, 128), F32),
        "go": pltpu.SemaphoreType.REGULAR,
        "load": pltpu.SemaphoreType.DMA((len(LOADED),)),
        "send": pltpu.SemaphoreType.DMA((len(SEM),)),
        "recv": pltpu.SemaphoreType.DMA((len(SEM),)),
    }
    names = list(large) + ["out"] + list(scratch)
    return pl.pallas_call(
        functools.partial(kernel, dims, names),
        out_shape=jax.ShapeDtypeStruct((rows_out, out_width), BF16),
        in_specs=[pl.BlockSpec(memory_space=pl.ANY)] * len(large),
        out_specs=pl.BlockSpec(memory_space=pltpu.VMEM),
        scratch_shapes=list(scratch.values()),
        compiler_params=pltpu.CompilerParams(
            collective_id=0, has_side_effects=True, vmem_limit_bytes=60 * 2**20
        ),
    )(*large.values())


def solution(mesh):
    return jax.shard_map(
        on_device,
        mesh=mesh,
        in_specs=(
            P("nodes", None),
            P(),
            P("nodes", "heads", None),
            P("heads", "nodes"),
            P("nodes", None, "heads", None),
            P("nodes", None, "heads", None),
            P("nodes", None, "heads", None),
            P("nodes", None, "heads", None),
            P(),
            P(),
            P(),
            P(),
            P(),
            P(),
        ),
        out_specs=P("heads", "nodes"),
        check_vma=False,
    )
```

time: 72.4 us -> 71.4 us (0.986)
  Pallas kernels: 71 us -> 69.9 us
    pallas_call x1, Pallas kernels: 71 us -> 69.9 us  [on_device(): pl.pallas_call(functools.partial(kernel, dims, names), out_shape=jax.Shap...]
where the time goes in v4:
time: 71.4 us; the launch traced here: 71.2 us
  Pallas kernels  69.9 us (98%)
  local copies, waits for them, and re-layouts  1.26 us (2%)
    pallas_call x1, Pallas kernels, on_device(): pl.pallas_call(functools.partial(kernel, dims, names), out_shape=jax.Shap...  69.9 us

profile of v4, /device:TPU:1, one launch (start us, length us, event | category | flops | bytes accessed | tf_op | source)
XLA Modules:
  0.0 71.2 jit_solution(13908734051864515124)
XLA Ops:
  0.0 69.9 %shard_map.136 = bf16[8,112]{1,0:T(8,128)(2,1)} custom-call(bf16[1,7168]{1,0:T(2,128)(2,1)} %refs_0_.1, f32[1,7168]{1,0:T(1,128)} %bitcast.23, s32[1,256]{1,0:T(1,128)} %bitcast.24, s32[1,32]{1,0:T(1,128)} %bitcast.25, s32[1,64]{1,0:T(1,128)} %bitcast.26, s32[1,64]{1,0:T(1,128)} %bitcast.27, s32[1,64]{1,0:T(1,128)} %bitcast.28, s32[1,64]{1,0:T(1,128)} %bitcast.29, ...), custom_call_target="tpu_custom_call" | custom-call | tf_op jit(solution)/shard_map/pallas_call | solution.py:594
  69.9 1.3 %copy.16 = bf16[8,112]{1,0:T(8,128)(2,1)} copy(bf16[8,112]{1,0:T(8,128)(2,1)} %shard_map.136) | data formatting | bytes 3584

commit v5 on v4

--- a/solution.py
+++ b/solution.py
@@ -19,7 +19,7 @@
     n: i
     for i, n in enumerate(
         ("rows", "twin", "nq0", "nq1", "fq", "qa0", "qa1", "xkv0", "xkv1", "nkv", "fkv", "leaf")
-        + ("xst0", "xst1", "xn0", "xn1", "fs", "fn0", "fn1", "aa0", "aa1", "out")
+        + ("xst0", "xst1", "xn0", "xn1", "fs0", "fs1", "fn0", "fn1", "aa0", "aa1", "out")
     )
 }
 ZS = 16
@@ -239,6 +239,18 @@
 
     for h in range(heads):
         pkv[:, h, :] = dot(lhs, r["w"][h, :, pl.ds(head_size, 2 * head_size)])
+    pkv16 = r["pkv16"]
+    pkv16[...] = pkv[...].astype(BF16)
+
+    xkv, skv, nkv, tkv, fkv = r["xkv"], r["skv"], r["nkv"], r["tkv"], r["fkv"]
+    row = pl.ds(x * ZS, ZS)
+    for dx in range(1, xs):
+        tx = across(dx)
+        remote(pkv16.at[pl.ds(tx * ZS, ZS)], xkv.at[core, dx - 1], SEM["xkv0"] + core, at(tx, z, hub))
+
+    @on_low
+    def _():
+        remote(pkv16.at[row], xkv.at[0, xs - 1], "xkv0", at(x, z, hub))
 
     @on_hub
     def _():
@@ -249,21 +261,6 @@
         fq[turn, 0] = jnp.sum(nq[0], axis=0)
         for tz in distant:
             remote(fq.at[turn], fq.at[turn], "fq", at(x, tz, hd))
-        pl.semaphore_signal(r["go"], inc=1, device_id=at(x, z, low), device_id_type=MESH)
-
-    @on_low
-    def _():
-        pl.semaphore_wait(r["go"], 1)
-
-    xkv, skv, nkv, tkv, fkv = r["xkv"], r["skv"], r["nkv"], r["tkv"], r["fkv"]
-    row = pl.ds(x * ZS, ZS)
-    for dx in range(1, xs):
-        tx = across(dx)
-        remote(pkv.at[pl.ds(tx * ZS, ZS)], xkv.at[core, dx - 1], SEM["xkv0"] + core, at(tx, z, hub))
-
-    @on_low
-    def _():
-        remote(pkv.at[row], xkv.at[0, xs - 1], "xkv0", at(x, z, hub))
 
     qa, q0 = r["qa"], r["q0"]
     row_ids = lax.broadcasted_iota(jnp.int32, (8, 1), 0)
@@ -291,7 +288,14 @@
 
     @on_hub
     def _():
-        xkv[1, xs - 1] = pkv[row]
+        xkv[1, xs - 1] = pkv16[row]
+        arrive("xkv1", xkv.at[1, three])
+        arrive("xkv0", xkv.at[0])
+        for p in range(2):
+            skv[:, p] = jnp.sum(xkv[p].astype(F32), axis=0)
+        for i, dz in enumerate((2, 1, -1)):
+            tz = lax.rem(z + dz + ZS, ZS)
+            remote(skv.at[pl.ds(lax.rem(tz, 4) * 4, 4)], nkv.at[i], "nkv", at(x, tz, hd))
         arrive("fq", fq.at[three])
 
         q0[...] = (fq[0, 0] + fq[1, 0] + fq[2, 0] + fq[3, 0]).astype(BF16)
@@ -304,13 +308,6 @@
             remote(qa.at[owned], qa.at[owned], "qa1", at(tx, tz, hd))
 
         remote(q0, qa.at[owned], "qa0", at(x, z, low))
-        arrive("xkv1", xkv.at[1, three])
-        arrive("xkv0", xkv.at[0])
-        for p in range(2):
-            skv[:, p] = jnp.sum(xkv[p], axis=0)
-        for i, dz in enumerate((2, 1, -1)):
-            tz = lax.rem(z + dz + ZS, ZS)
-            remote(skv.at[pl.ds(lax.rem(tz, 4) * 4, 4)], nkv.at[i], "nkv", at(x, tz, hd))
         leaf_part(1)
         arrive("nkv", nkv)
         tkv[...] = skv[pl.ds(lax.rem(z, 4) * 4, 4)] + jnp.sum(nkv[...], axis=0)
@@ -399,60 +396,56 @@
         xst[1, near] = st[block]
         xn[1, near] = nb[owned]
         arrive("fkv", fkv)
-        extras = {1: extra_of(1)}
-        factors, extra_f = {}, {}
+        extras = extra_of(1)
         for p in (1, 0):
-            if p:
-                arrive("xst1", xst.at[1, fifteen])
-            else:
-                arrive("leaf", leaf.at[0])
-                extras[0] = extra_of(0)
-                arrive("xst0", xst.at[0])
-            stats, extra = xst[p, :, 0, :], extras[p][0]
+            arrive("xst1" if p else "xst0", xst.at[1, fifteen] if p else xst.at[0])
+            stats, (extra, extra_n) = xst[p, :, 0, :], extras
             top = jnp.maximum(jnp.max(stats, axis=0, keepdims=True), extra)
-            factors[p] = jnp.exp(stats - top)
-            extra_f[p] = jnp.where(my_maxima, jnp.exp(extra - top), 0.0)
-            total = jnp.sum(onward(factors[p]) * stats, axis=0, keepdims=True)
-            total = total + onward(extra_f[p]) * extra
+            factors = jnp.exp(stats - top)
+            extra_f = jnp.where(my_maxima, jnp.exp(extra - top), 0.0)
+            total = jnp.sum(onward(factors) * stats, axis=0, keepdims=True)
+            total = total + onward(extra_f) * extra
             fs[turn, p] = jnp.where(maximum_lane, top, total)
-        for tz in distant:
-            remote(fs.at[turn], fs.at[turn], "fs", at(x, tz, hd))
-        for p in (1, 0):
-            if p:
-                arrive("xn1", xn.at[1, fifteen])
-            else:
-                arrive("xn0", xn.at[0])
+            for tz in distant:
+                remote(fs.at[turn, p], fs.at[turn, p], "fs1" if p else "fs0", at(x, tz, hd))
+            arrive("xn1" if p else "xn0", xn.at[1, fifteen] if p else xn.at[0])
             for i in range(4):
-                summed = upright(extra_f[p], i) * extras[p][1]
+                summed = upright(extra_f, i) * extra_n
                 for s in range(near + 1):
-                    summed = summed + upright(factors[p][s : s + 1], i) * xn[p, s, i].astype(F32)
+                    summed = summed + upright(factors[s : s + 1], i) * xn[p, s, i].astype(F32)
                 fn[turn, p, i] = summed.astype(BF16)
             for tz in distant:
                 remote(fn.at[turn, p], fn.at[turn, p], "fn1" if p else "fn0", at(x, tz, hd))
-        arrive("fs", fs.at[three])
-        for p in (0, 1):
+            if p:
+                arrive("leaf", leaf.at[0])
+                extras = extra_of(0)
+
+        for p in (1, 0):
+            arrive("fs1" if p else "fs0", fs.at[three, p])
             stats = fs[:, p, 0, :]
             top = jnp.max(stats, axis=0, keepdims=True)
             f = jnp.exp(stats - top)
             total = pltpu.roll(jnp.sum(onward(f) * stats, axis=0, keepdims=True), 120, 1)
             f = f / jnp.where(maximum_lane & (lane < 64), total, 1.0)
-            factors[p] = [[upright(f[s : s + 1], i) for s in range(4)] for i in range(4)]
-        arrive("fn1", fn.at[three, 1])
-        arrive("fn0", fn.at[three, 0])
-
-        for p in (0, 1):
+            f = [[upright(f[s : s + 1], i) for s in range(4)] for i in range(4)]
+            arrive("fn1" if p else "fn0", fn.at[three, p])
             for i in range(4):
-                attended = sum(factors[p][i][s] * fn[s, p, i].astype(F32) for s in range(4))
+                attended = sum(f[i][s] * fn[s, p, i].astype(F32) for s in range(4))
                 if p:
                     aa[block * 4 + i] = attended.astype(BF16)
                 else:
                     a0[i] = attended.astype(BF16)
+            if p:
+
+                @pl.loop(0, near)
+                def _(j):
+                    tx, tz = neighbour(j)
+                    remote(aa.at[owned], aa.at[owned], "aa1", at(tx, tz, hd))
 
         @pl.loop(0, near)
         def _(j):
             tx, tz = neighbour(j)
             remote(a0, aa.at[owned], "aa0", at(tx, tz, low))
-            remote(aa.at[owned], aa.at[owned], "aa1", at(tx, tz, hd))
 
         remote(a0, aa.at[owned], "aa0", at(x, z, low))
 
@@ -504,7 +497,8 @@
         left("fkv", fkv)
         left("xst1", xst.at[1, fifteen])
         left("xn1", xn.at[1, fifteen])
-        left("fs", fs.at[three])
+        left("fs0", fs.at[three, 0])
+        left("fs1", fs.at[three, 1])
         left("fn0", fn.at[three, 0])
         left("fn1", fn.at[three, 1])
         left("aa0", aa)
@@ -564,7 +558,8 @@
         "nq": vmem((2, xs * 4, 4, 8, head_size), F32),
         "fq": vmem((4, 2, 4, 8, head_size), F32),
         "pkv": vmem((nodes, 8, 2 * head_size), F32),
-        "xkv": vmem((2, xs, ZS, 8, 2 * head_size), F32),
+        "pkv16": vmem((nodes, 8, 2 * head_size), BF16),
+        "xkv": vmem((2, xs, ZS, 8, 2 * head_size), BF16),
         "skv": vmem((ZS, 2, 8, 2 * head_size), F32),
         "nkv": vmem((3, 4, 2, 8, 2 * head_size), F32),
         "tkv": vmem((4, 2, 8, 2 * head_size), F32),
@@ -585,7 +580,6 @@
         "fs": vmem((4, 2, 1, 128), F32),
         "os": vmem((heads_n, rows_out, 128), F32),
         "orr": vmem((heads_n - 1, rows_out, 128), F32),
-        "go": pltpu.SemaphoreType.REGULAR,
         "load": pltpu.SemaphoreType.DMA((len(LOADED),)),
         "send": pltpu.SemaphoreType.DMA((len(SEM),)),
         "recv": pltpu.SemaphoreType.DMA((len(SEM),)),

time: 71.4 us -> 70.1 us (0.982)
  Pallas kernels: 69.9 us -> 68.6 us
    pallas_call x1, Pallas kernels: 69.9 us -> 68.6 us  [on_device(): pl.pallas_call(functools.partial(kernel, dims, names), out_shape=jax.Shap...]
where the time goes in v5:
time: 70.1 us; the launch traced here: 69.9 us
  Pallas kernels  68.6 us (98%)
  local copies, waits for them, and re-layouts  1.26 us (2%)
    pallas_call x1, Pallas kernels, on_device(): pl.pallas_call(functools.partial(kernel, dims, names), out_shape=jax.Shap...  68.6 us

profile of v5, /device:TPU:1, one launch (start us, length us, event | category | flops | bytes accessed | tf_op | source)
XLA Modules:
  0.0 69.9 jit_solution(4760580515820949332)
XLA Ops:
  0.0 68.6 %shard_map.136 = bf16[8,112]{1,0:T(8,128)(2,1)} custom-call(bf16[1,7168]{1,0:T(2,128)(2,1)} %refs_0_.1, f32[1,7168]{1,0:T(1,128)} %bitcast.23, s32[1,256]{1,0:T(1,128)} %bitcast.24, s32[1,32]{1,0:T(1,128)} %bitcast.25, s32[1,64]{1,0:T(1,128)} %bitcast.26, s32[1,64]{1,0:T(1,128)} %bitcast.27, s32[1,64]{1,0:T(1,128)} %bitcast.28, s32[1,64]{1,0:T(1,128)} %bitcast.29, ...), custom_call_target="tpu_custom_call" | custom-call | tf_op jit(solution)/shard_map/pallas_call | solution.py:588
  68.6 1.3 %copy.16 = bf16[8,112]{1,0:T(8,128)(2,1)} copy(bf16[8,112]{1,0:T(8,128)(2,1)} %shard_map.136) | data formatting | bytes 3584

commit v6 on v5

--- a/solution.py
+++ b/solution.py
@@ -18,7 +18,7 @@
 SEM = {
     n: i
     for i, n in enumerate(
-        ("rows", "twin", "nq0", "nq1", "fq", "qa0", "qa1", "xkv0", "xkv1", "nkv", "fkv", "leaf")
+        ("rows", "twin", "nq0", "nq1", "fq0", "fq1", "qa0", "qa1", "xkv0", "xkv1", "nkv", "fkv", "leaf")
         + ("xst0", "xst1", "xn0", "xn1", "fs0", "fs1", "fn0", "fn1", "aa0", "aa1", "out")
     )
 }
@@ -257,10 +257,12 @@
         nq[1, near] = pq[owned]
         arrive("nq1", nq.at[1, fifteen])
         fq[turn, 1] = jnp.sum(nq[1], axis=0)
+        for tz in distant:
+            remote(fq.at[turn, 1], fq.at[turn, 1], "fq1", at(x, tz, hd))
         arrive("nq0", nq.at[0])
         fq[turn, 0] = jnp.sum(nq[0], axis=0)
         for tz in distant:
-            remote(fq.at[turn], fq.at[turn], "fq", at(x, tz, hd))
+            remote(fq.at[turn, 0], fq.at[turn, 0], "fq0", at(x, tz, hd))
 
     qa, q0 = r["qa"], r["q0"]
     row_ids = lax.broadcasted_iota(jnp.int32, (8, 1), 0)
@@ -296,16 +298,22 @@
         for i, dz in enumerate((2, 1, -1)):
             tz = lax.rem(z + dz + ZS, ZS)
             remote(skv.at[pl.ds(lax.rem(tz, 4) * 4, 4)], nkv.at[i], "nkv", at(x, tz, hd))
-        arrive("fq", fq.at[three])
-
+        arrive("fq1", fq.at[three, 1])
+
+        qa[owned] = (fq[0, 1] + fq[1, 1] + fq[2, 1] + fq[3, 1]).astype(BF16)
+
+        @pl.loop(0, near)
+        def _(j):
+            tx, tz = neighbour(j)
+            remote(qa.at[owned], qa.at[owned], "qa1", at(tx, tz, hd))
+
+        arrive("fq0", fq.at[three, 0])
         q0[...] = (fq[0, 0] + fq[1, 0] + fq[2, 0] + fq[3, 0]).astype(BF16)
-        qa[owned] = (fq[0, 1] + fq[1, 1] + fq[2, 1] + fq[3, 1]).astype(BF16)
 
         @pl.loop(0, near)
         def _(j):
             tx, tz = neighbour(j)
             remote(q0, qa.at[owned], "qa0", at(tx, tz, low))
-            remote(qa.at[owned], qa.at[owned], "qa1", at(tx, tz, hd))
 
         remote(q0, qa.at[owned], "qa0", at(x, z, low))
         leaf_part(1)
@@ -489,7 +497,8 @@
         left("rows", cols.at[pl.ds(0, nodes - 1)])
         left("twin", cols)
         left("nq1", nq.at[1, fifteen])
-        left("fq", fq.at[three])
+        left("fq0", fq.at[three, 0])
+        left("fq1", fq.at[three, 1])
         left("qa0", qa)
         left("qa1", qa.at[pl.ds(0, near * 4)])
         left("xkv1", xkv.at[1, three])

time: 70.1 us -> 68.3 us (0.974)
  Pallas kernels: 68.6 us -> 66.8 us
    pallas_call x1, Pallas kernels: 68.6 us -> 66.8 us  [on_device(): pl.pallas_call(functools.partial(kernel, dims, names), out_shape=jax.Shap...]
where the time goes in v6:
time: 68.3 us; the launch traced here: 68.1 us
  Pallas kernels  66.8 us (98%)
  local copies, waits for them, and re-layouts  1.26 us (2%)
    pallas_call x1, Pallas kernels, on_device(): pl.pallas_call(functools.partial(kernel, dims, names), out_shape=jax.Shap...  66.8 us

profile of v6, /device:TPU:1, one launch (start us, length us, event | category | flops | bytes accessed | tf_op | source)
XLA Modules:
  0.0 68.1 jit_solution(1504265384745188876)
XLA Ops:
  0.0 66.8 %shard_map.136 = bf16[8,112]{1,0:T(8,128)(2,1)} custom-call(bf16[1,7168]{1,0:T(2,128)(2,1)} %refs_0_.1, f32[1,7168]{1,0:T(1,128)} %bitcast.23, s32[1,256]{1,0:T(1,128)} %bitcast.24, s32[1,32]{1,0:T(1,128)} %bitcast.25, s32[1,64]{1,0:T(1,128)} %bitcast.26, s32[1,64]{1,0:T(1,128)} %bitcast.27, s32[1,64]{1,0:T(1,128)} %bitcast.28, s32[1,64]{1,0:T(1,128)} %bitcast.29, ...), custom_call_target="tpu_custom_call" | custom-call | tf_op jit(solution)/shard_map/pallas_call | solution.py:597
  66.8 1.3 %copy.16 = bf16[8,112]{1,0:T(8,128)(2,1)} copy(bf16[8,112]{1,0:T(8,128)(2,1)} %shard_map.136) | data formatting | bytes 3584

commit v7 on v6

--- a/solution.py
+++ b/solution.py
@@ -244,12 +244,11 @@
 
     xkv, skv, nkv, tkv, fkv = r["xkv"], r["skv"], r["nkv"], r["tkv"], r["fkv"]
     row = pl.ds(x * ZS, ZS)
-    for dx in range(1, xs):
-        tx = across(dx)
-        remote(pkv16.at[pl.ds(tx * ZS, ZS)], xkv.at[core, dx - 1], SEM["xkv0"] + core, at(tx, z, hub))
-
-    @on_low
-    def _():
+    @on_low
+    def _():
+        for dx in range(1, xs):
+            tx = across(dx)
+            remote(pkv16.at[pl.ds(tx * ZS, ZS)], xkv.at[0, dx - 1], "xkv0", at(tx, z, hub))
         remote(pkv16.at[row], xkv.at[0, xs - 1], "xkv0", at(x, z, hub))
 
     @on_hub
@@ -259,6 +258,9 @@
         fq[turn, 1] = jnp.sum(nq[1], axis=0)
         for tz in distant:
             remote(fq.at[turn, 1], fq.at[turn, 1], "fq1", at(x, tz, hd))
+        for dx in range(1, xs):
+            tx = across(dx)
+            remote(pkv16.at[pl.ds(tx * ZS, ZS)], xkv.at[1, dx - 1], "xkv1", at(tx, z, hd))
         arrive("nq0", nq.at[0])
         fq[turn, 0] = jnp.sum(nq[0], axis=0)
         for tz in distant:

time: 68.3 us -> 68.2 us (level)
  no operation moved by 1% of the time
where the time goes in v7:
time: 68.2 us; the launch traced here: 68 us
  Pallas kernels  66.7 us (98%)
  local copies, waits for them, and re-layouts  1.26 us (2%)
    pallas_call x1, Pallas kernels, on_device(): pl.pallas_call(functools.partial(kernel, dims, names), out_shape=jax.Shap...  66.7 us

profile of v7, /device:TPU:1, one launch (start us, length us, event | category | flops | bytes accessed | tf_op | source)
XLA Modules:
  0.0 68.0 jit_solution(2897211705930245708)
XLA Ops:
  0.0 66.7 %shard_map.136 = bf16[8,112]{1,0:T(8,128)(2,1)} custom-call(bf16[1,7168]{1,0:T(2,128)(2,1)} %refs_0_.1, f32[1,7168]{1,0:T(1,128)} %bitcast.23, s32[1,256]{1,0:T(1,128)} %bitcast.24, s32[1,32]{1,0:T(1,128)} %bitcast.25, s32[1,64]{1,0:T(1,128)} %bitcast.26, s32[1,64]{1,0:T(1,128)} %bitcast.27, s32[1,64]{1,0:T(1,128)} %bitcast.28, s32[1,64]{1,0:T(1,128)} %bitcast.29, ...), custom_call_target="tpu_custom_call" | custom-call | tf_op jit(solution)/shard_map/pallas_call | solution.py:599
  66.7 1.3 %copy.16 = bf16[8,112]{1,0:T(8,128)(2,1)} copy(bf16[8,112]{1,0:T(8,128)(2,1)} %shard_map.136) | data formatting | bytes 3584
